TPU v7x, 256 devices: a whole 4x4x8 slice. The times are simulated.
256 devices in a mesh: seq: 64 (over z, x, core), head: 4 (over y).
Axes of the slice: x: 4, y: 4, z: 8, core: 2. Of those that a mesh axis runs over, the one named last changes fastest.
Arguments:
- queries: bfloat16 [8192, 4096], P('seq', 'head'), may hold values from -6 to 6, as said below
- keys: bfloat16 [8192, 4096], P('seq', 'head'), may hold values from -6 to 6, as said below
- values: bfloat16 [8192, 4096], P('seq', 'head'), may hold values from -6 to 6
- transitions: bfloat16 [8192, 4096], P('seq', 'head'), may hold values from -6 to 6, as said below
- betas: bfloat16 [8192, 32], P('seq', 'head'), may hold values from 0.19921875 to 1.5
- segments: int32 [8192], replicated, may hold values from 0 to 15, never falling along the last dimension, each value on 1 to 1024 neighbouring positions
- visits: int32 [64, 3], P('seq'), may hold values 0 or 1
Outputs:
- attended: bfloat16 [8192, 4096], P('seq', 'head')
Inputs may be any that keep to these rules, and one draw needn't show every extreme that they name: `queries`: real-valued entries. `keys`: real-valued entries. `transitions`: real-valued entries, no head row all zero.
All inputs are finite; a program needn't handle non-finite values. No bound on the sum of `visits` on one device may be relied on, other than what follows from the above.
Results may differ from a plain program's by a relative error of at most 0.0036.
Values may be sent and summed in bfloat16 or wider, within the bound.
No kernel may reach another device: no remote copies, remote signals or barrier semaphores. Data moves between devices by JAX's collectives and lax.ppermute only.
A program may use at most 64 MiB of HBM per device.

v0:
```python
import jax
import jax.numpy as jnp
from jax import lax
from jax.sharding import PartitionSpec as P

HEAD_DIM = 128
BACK = 3


HIGHEST = lax.Precision.HIGHEST
EPSILON = 1e-06


def passed_along(value, axis, by):
    size = lax.axis_size(axis)
    pairs = [(i, i + by) for i in range(size) if 0 <= i + by < size]
    return lax.ppermute(value, axis, pairs)


def heads_first(block, head_count):
    height = block.shape[0]
    return jnp.transpose(block.reshape(height, head_count, -1), (1, 0, 2))


def paired_product(left, right):
    return jnp.einsum("hpab,hpbc->hpac", left, right, precision=HIGHEST)


def diagonal_blocks(matrix, size):
    heads = matrix.shape[0]
    count = matrix.shape[1] // size
    blocks = jnp.diagonal(matrix.reshape(heads, count, size, count, size), axis1=1, axis2=3)
    return jnp.transpose(blocks, (0, 3, 1, 2))


def unit_inverse(lower_mat):
    length = lower_mat.shape[1]
    base = min(16, length)
    blocks = diagonal_blocks(lower_mat, base)
    identity = jnp.eye(base, dtype=jnp.float32)
    nilpotent = blocks - identity
    inverse = identity - nilpotent
    power = nilpotent
    reach = 2
    while reach < base:
        power = paired_product(power, power)
        inverse = paired_product(inverse, identity + power)
        reach = reach * 2
    size = base
    while size < length:
        joined = diagonal_blocks(lower_mat, 2 * size)
        lower_left = joined[:, :, size:, :size]
        first = inverse[:, 0::2]
        second = inverse[:, 1::2]
        corner = -paired_product(second, paired_product(lower_left, first))
        upper = jnp.concatenate([first, jnp.zeros_like(first)], axis=-1)
        bottom = jnp.concatenate([corner, second], axis=-1)
        inverse = jnp.concatenate([upper, bottom], axis=-2)
        size = size * 2
    return inverse[:, 0]


def transition_parts(key_rows, raw_w, strength):
    length = key_rows.shape[1]
    width = key_rows.shape[2]
    unit_w = raw_w / jnp.sqrt(jnp.sum(raw_w * raw_w, axis=-1, keepdims=True) + EPSILON)
    strict = jnp.tril(jnp.ones((length, length), jnp.float32), -1)
    gram_mat = jnp.einsum("htd,hsd->hts", unit_w, unit_w, precision=HIGHEST)
    lower_mat = (
        jnp.eye(length, dtype=jnp.float32)[None] + strict[None] * strength[:, :, None] * gram_mat
    )
    cross_terms = jnp.einsum("htd,hjd->htj", unit_w, key_rows, precision=HIGHEST)
    right_side = jnp.concatenate(
        [strength[:, :, None] * unit_w, strict[None] * strength[:, :, None] * cross_terms], axis=-1
    )
    solved = jnp.einsum("hts,hsc->htc", unit_inverse(lower_mat), right_side, precision=HIGHEST)
    back_rows = solved[:, :, :width]
    carry_coef = solved[:, :, width:]
    carried = key_rows - jnp.einsum("htj,htd->hjd", carry_coef, unit_w, precision=HIGHEST)
    return (unit_w, back_rows, carry_coef, carried)


def query_parts(query_half, key_half, query_rows, unit_w, back_rows, carry_coef):
    length = query_rows.shape[1]
    inclusive = jnp.tril(jnp.ones((length, length), jnp.float32))
    query_w = jnp.einsum("hid,htd->hit", query_rows, unit_w, precision=HIGHEST) * inclusive[None]
    turned = query_rows - jnp.einsum("hit,htd->hid", query_w, back_rows, precision=HIGHEST)
    own_scores = jnp.einsum(
        "hid,hjd->hij", query_half, key_half, preferred_element_type=jnp.float32
    )
    own_scores = own_scores - jnp.einsum("hit,htj->hij", query_w, carry_coef, precision=HIGHEST)
    return (turned, own_scores)


def advance(carried, back_rows, unit_w):
    inner = jnp.einsum("hjd,htd->hjt", carried, back_rows, precision=HIGHEST)
    return carried - jnp.einsum("hjt,htd->hjd", inner, unit_w, precision=HIGHEST)


def weights_of(turned, own_scores, far_keys, seg_keys, seg_query, visit_row):
    length = own_scores.shape[1]
    cross_terms = jnp.einsum("hid,hjd->hij", turned, far_keys, precision=HIGHEST)
    scores = jnp.concatenate([cross_terms, own_scores], axis=-1) * HEAD_DIM ** (-0.5)
    spread = scores.shape[2]
    visited = jnp.concatenate([visit_row[::-1], jnp.ones((1,), jnp.int32)])
    visited = jnp.repeat(visited, length, total_repeat_length=spread)
    column = jnp.arange(spread, dtype=jnp.int32)
    row_ids = jnp.arange(length, dtype=jnp.int32)
    allowed = (visited[None, :] > 0) & (seg_keys[None, :] == seg_query[:, None])
    allowed = allowed & (column[None, :] <= row_ids[:, None] + (spread - length))
    scores = jnp.where(allowed[None], scores, -1e30)
    row_max = jnp.max(scores, axis=-1, keepdims=True)
    weights = jnp.exp(scores - row_max)
    total_w = jnp.sum(weights, axis=-1, keepdims=True)
    return (weights.astype(jnp.bfloat16), total_w)


def shards(queries, keys, values, transitions, betas, segments, visits):
    length = queries.shape[0]
    head_count = betas.shape[1]
    key_half = heads_first(keys, head_count)
    query_half = heads_first(queries, head_count)
    key_rows = key_half.astype(jnp.float32)
    unit_w, back_rows, carry_coef, carried = transition_parts(
        key_rows,
        heads_first(transitions.astype(jnp.float32), head_count),
        betas.astype(jnp.float32).T,
    )
    turned, own_scores = query_parts(
        query_half, key_half, query_half.astype(jnp.float32), unit_w, back_rows, carry_coef
    )
    far_list = []
    value_list = []
    moving = carried
    moving_vals = values
    for distance in range(BACK):
        moving = passed_along(moving, "seq", 1)
        moving_vals = passed_along(moving_vals, "seq", 1)
        far_list.insert(0, moving)
        value_list.insert(0, moving_vals)
        if distance + 1 < BACK:
            moving = advance(moving, back_rows, unit_w)
    far_keys = jnp.concatenate(far_list, axis=1)
    value_rows = jnp.concatenate(value_list + [values], axis=0)
    block_id = lax.axis_index("seq")
    padding = jnp.full((BACK * length,), -1, jnp.int32)
    seg_keys = lax.dynamic_slice_in_dim(
        jnp.concatenate([padding, segments]), block_id * length, (BACK + 1) * length
    )
    weights, total_w = weights_of(
        turned, own_scores, far_keys, seg_keys, seg_keys[BACK * length :], visits[0]
    )
    mixed = (
        jnp.einsum(
            "hij,hjd->hid",
            weights,
            heads_first(value_rows, head_count),
            preferred_element_type=jnp.float32,
        )
        / total_w
    )
    return jnp.transpose(mixed, (1, 0, 2)).reshape(length, -1).astype(jnp.bfloat16)


def solution(mesh):
    return jax.shard_map(
        shards,
        mesh=mesh,
        in_specs=(
            P("seq", "head"),
            P("seq", "head"),
            P("seq", "head"),
            P("seq", "head"),
            P("seq", "head"),
            P(),
            P("seq", None),
        ),
        out_specs=P("seq", "head"),
        check_vma=False,
    )
```

profile of v0, /device:TPU:136, one launch (start us, length us, event | category | flops | bytes accessed | tf_op | source)
XLA Modules:
  0.0 93.2 jit_solution(14995542900860645033)
XLA Ops:
  0.0 1.2 %copy.22 = bf16[128,1024]{0,1:T(8,128)(2,1)S(1)} copy(bf16[128,1024]{1,0:T(8,128)(2,1)} %param.12) | data formatting | bytes 524288 | tf_op args[3]
  1.2 0.1 copy.23
  1.4 0.2 fusion.32
  1.6 0.7 convert_bitcast_fusion
  2.4 1.3 %fusion.9 = f32[8,128,128]{2,1,0:T(8,128)S(1)} fusion(f32[8,128]{1,0:T(8,128)S(1)} %convert_bitcast_fusion, f32[128,128]{1,0:T(8,128)S(1)} %copy.24, f32[128,128]{1,0:T(8,128)S(1)} %fusion.71, f32[128,8,128]{2,0,1:T(8,128)S(1)} %copy.23, f32[8,128]{1,0:T(8,128)S(1)} %add_sqrt_fusion), kind=kOutput, calls=%fused_computation.24 | convolution fusion | flops 201850880 | bytes 1187840 | tf_op jit(solution)/shard_map/htd,hsd->hts/dot_general | solution.py:68
  3.7 2.6 %reshape.258 = f32[8,8,16,8,16]{4,3,2,1,0:T(8,128)} reshape(f32[8,128,128]{2,1,0:T(8,128)S(1)} %fusion.9) | data formatting | bytes 1048576 | tf_op jit(solution)/shard_map/reshape | solution.py:32
  6.3 5.1 %copy.81 = f32[8,8,16,8,16]{4,2,3,1,0:T(8,128)} copy(f32[8,8,16,8,16]{4,3,2,1,0:T(8,128)} %reshape.258) | data formatting | bytes 1048576 | tf_op jit(solution)/shard_map/reshape | solution.py:32
  11.4 2.8 %gather_fusion = f32[8,8,16,16]{3,2,1,0:T(8,128)S(1)} fusion(f32[8,16,16,8,8]{2,1,4,3,0:T(8,128)} %bitcast.128, s32[8]{0:T(128)S(1)} %or_bitcast_fusion.2), kind=kCustom, calls=%fused_computation | custom fusion | bytes 131136 | tf_op jit(solution)/shard_map/jit(diagonal)/gather | solution.py:32
  14.1 0.6 fusion.40
  14.8 0.7 fusion.35
  15.5 0.6 fusion.91
  16.1 2.3 %reshape.259 = f32[8,4,32,4,32]{4,3,2,1,0:T(4,128)} reshape(f32[8,128,128]{2,1,0:T(8,128)S(1)} %fusion.9) | data formatting | bytes 1048576 | tf_op jit(solution)/shard_map/reshape | solution.py:32
  18.4 1.6 %reshape.260 = f32[8,2,64,2,64]{4,3,2,1,0:T(2,128)} reshape(f32[8,128,128]{2,1,0:T(8,128)S(1)} %fusion.9) | data formatting | bytes 1048576 | tf_op jit(solution)/shard_map/reshape | solution.py:32
  20.0 1.2 %broadcast_multiply_fusion = f32[8,128,128]{2,1,0:T(8,128)} fusion(f32[8,128]{1,0:T(8,128)S(1)} %convert_bitcast_fusion, f32[8,128]{1,0:T(8,128)S(1)} %add_sqrt_fusion, f32[128,8,128]{2,0,1:T(8,128)S(1)} %copy.23), kind=kLoop, calls=%fused_computation.93 | loop fusion | flops 262144 | bytes 1056768 | tf_op jit(solution)/shard_map/mul | solution.py:74
  21.1 0.6 convolution_add_fusion
  21.8 0.7 fusion.33
  22.5 0.7 convolution_bitcast_fusion.2
  23.1 0.8 copy-done.5
  23.9 0.8 fusion.89
  24.7 0.3 copy.82
  25.0 0.6 gather_fusion.1
  25.6 1.4 %fusion.61 = f32[8,4,16,16]{3,2,1,0:T(8,128)S(1)} fusion(f32[8,4,16,16]{3,2,0,1:T(8,128)} %get-tuple-element.22, f32[8,4,32,32]{3,2,0,1:T(8,128)S(1)} %bitcast.126), kind=kOutput, calls=%fused_computation.87 | convolution fusion | flops 1572864 | bytes 327680 | tf_op jit(solution)/shard_map/hpab,hpbc->hpac/dot_general | solution.py:26
  27.0 1.3 %convolution_negate_fusion.2 = f32[8,4,16,16]{3,2,0,1:T(8,128)S(1)} fusion(f32[8,4,16,16]{3,2,1,0:T(8,128)S(1)} %fusion.61, f32[8,8,16,16]{3,2,0,1:T(8,128)} %copy-done.5), kind=kOutput, calls=%fused_computation.32 | convolution fusion | flops 1581056 | bytes 327680 | tf_op jit(solution)/shard_map/hpab,hpbc->hpac/dot_general | solution.py:26
  28.4 1.2 %select_maximum_fusion.2 = f32[8,4,32,32]{3,2,0,1:T(8,128)S(1)} fusion(f32[8,4,16,16]{3,2,0,1:T(8,128)} %get-tuple-element.22, f32[8,4,16,16]{3,2,0,1:T(8,128)} %get-tuple-element.21, f32[8,4,16,16]{3,2,0,1:T(8,128)S(1)} %convolution_negate_fusion.2), kind=kLoop, calls=%fused_computation.49 | loop fusion | flops 131072 | bytes 229376 | tf_op jit(solution)/shard_map/concatenate | solution.py:58
  29.6 0.1 copy.83
  29.7 0.6 gather_fusion.2
  30.3 0.4 fusion.57
  30.7 0.4 convolution_negate_fusion.1
  31.1 0.1 select_maximum_fusion.1
  31.4 0.4 fusion.49
  31.8 0.4 fusion.11
  32.2 0.2 copy.32
  32.3 0.2 copy.33
  32.5 0.7 convolution_multiply_fusion.1
  33.2 1.1 %fusion.19 = f32[8,128,256]{2,1,0:T(8,128)S(1)} fusion(f32[8,128,128]{2,1,0:T(8,128)S(1)} %convolution_multiply_fusion.1, f32[8,128,128]{2,1,0:T(8,128)S(1)} %copy-done.6, f32[8,1,64,64]{3,2,0,1:T(8,128)S(1)} %get-tuple-element.18, f32[8,1,64,64]{3,2,0,1:T(8,128)S(1)} %get-tuple-element.17, f32[8,1,64,64]{3,2,0,1:T(8,128)S(1)} %fusion.11), kind=kOutput, calls=%fused_computation.35 | convolution fusion | flops 403439616 | bytes 2490368 | tf_op jit(solution)/shard_map/hts,hsc->htc/dot_general | solution.py:76
  34.3 1.3 %convolution_subtract_fusion.3 = f32[8,128,128]{2,1,0:T(8,128)S(1)} fusion(f32[8,128,256]{2,1,0:T(8,128)S(1)} %fusion.19, bf16[128,8,128]{2,0,1:T(8,128)(2,1)S(1)} %copy.33, f32[128,8,128]{2,0,1:T(8,128)S(1)} %copy.23, f32[8,128]{1,0:T(8,128)S(1)} %add_sqrt_fusion), kind=kOutput, calls=%fused_computation.20 | convolution fusion | flops 201719808 | bytes 1839104 | tf_op jit(solution)/shard_map/htj,htd->hjd/dot_general | solution.py:79
  35.7 1.9 %collective-permute-start = (f32[8,128,128]{2,1,0:T(8,128)S(1)}, f32[8,128,128]{2,1,0:T(8,128)S(1)}, u32[]{:S(2)}, u32[]{:S(2)}) collective-permute-start(f32[8,128,128]{2,1,0:T(8,128)S(1)} %convolution_subtract_fusion.3), channel_id=1, source_target_pairs={{0,4},{4,8},{8,12},{12,16},{16,20},{20,24},{24,28},{28,32},{32,36}... | collective-permute-start | bytes 1572872 | tf_op jit(solution)/shard_map/ppermute | solution.py:17
  37.6 3.5 %collective-permute-start.3 = (bf16[128,1024]{1,0:T(8,128)(2,1)}, bf16[128,1024]{1,0:T(8,128)(2,1)}, u32[]{:S(2)}, u32[]{:S(2)}) collective-permute-start(bf16[128,1024]{1,0:T(8,128)(2,1)} %param.11), channel_id=1, source_target_pairs={{0,4},{4,8},{8,12},{12,16},{16,20},{20,24},{24,28},{28,32},{32,36}... | collective-permute-start | bytes 786440 | tf_op jit(solution)/shard_map/ppermute | solution.py:17
  41.2 0.6 fusion.90
  41.9 2.0 %compare_select_fusion.1 = s32[512,1]{0,1:T(1,128)S(1)} fusion(s32[512,1]{0,1:T(1,128)S(1)} %bitcast.136, s32[512,1]{0,1:T(1,128)S(1)} %bitcast.135, s32[]{:T(128)} %bitcast.4, s32[]{:T(128)} %bitcast.6, s32[]{:T(128)} %bitcast.5), kind=kLoop, calls=%fused_computation.108 | loop fusion | flops 4096 | bytes 6156 | tf_op jit(solution)/shard_map/jit(_take)/gather | solution.py:106
  43.9 0.7 fusion.10
  44.6 4.9 %collective-permute-done = f32[8,128,128]{2,1,0:T(8,128)S(1)} collective-permute-done((f32[8,128,128]{2,1,0:T(8,128)S(1)}, f32[8,128,128]{2,1,0:T(8,128)S(1)}, u32[]{:S(2)}, u32[]{:S(2)}) %collective-permute-start) | collective-permute-done | bytes 524320 | tf_op jit(solution)/shard_map/ppermute | solution.py:17
  49.5 1.2 %fusion.45 = f32[8,128,128]{2,1,0:T(8,128)S(1)} fusion(f32[8,128,128]{2,1,0:T(8,128)S(1)} %collective-permute-done, f32[8,128,256]{2,1,0:T(8,128)S(1)} %fusion.19), kind=kOutput, calls=%fused_computation.69 | convolution fusion | flops 201326592 | bytes 1572864 | tf_op jit(solution)/shard_map/hjd,htd->hjt/dot_general | solution.py:96
  50.7 0.8 convolution_subtract_fusion.2
  51.5 1.9 %collective-permute-start.1 = (f32[8,128,128]{2,1,0:T(8,128)S(1)}, f32[8,128,128]{2,1,0:T(8,128)S(1)}, u32[]{:S(2)}, u32[]{:S(2)}) collective-permute-start(f32[8,128,128]{2,1,0:T(8,128)S(1)} %convolution_subtract_fusion.2), channel_id=1, source_target_pairs={{0,4},{4,8},{8,12},{12,16},{16,20},{20,24},{24,28},{28,32},{32,36}... | collective-permute-start | bytes 1572872 | tf_op jit(solution)/shard_map/ppermute | solution.py:17
  53.4 0.3 fusion.48
  53.7 1.0 %convolution_subtract_fusion = f32[8,128,128]{2,1,0:T(8,128)S(1)} fusion(f32[8,128,128]{2,1,0:T(8,128)S(1)} %fusion.48, f32[8,128,128]{1,2,0:T(8,128)S(1)} %fusion.10, f32[8,128,256]{2,1,0:T(8,128)S(1)} %fusion.19), kind=kOutput, calls=%fused_computation.17 | convolution fusion | flops 201457664 | bytes 2097152 | tf_op jit(solution)/shard_map/hit,htj->hij/dot_general | solution.py:91
  54.7 1.9 %collective-permute-start.4 = (bf16[128,1024]{1,0:T(8,128)(2,1)}, bf16[128,1024]{1,0:T(8,128)(2,1)S(1)}, u32[]{:S(2)}, u32[]{:S(2)}) collective-permute-start(bf16[128,1024]{1,0:T(8,128)(2,1)} %collective-permute-done.3), channel_id=1, source_target_pairs={{0,4},{4,8},{8,12},{12,16},{16,20},{20,24},{24,28},{28,32},{32,36}... | collective-permute-start | bytes 786440 | tf_op jit(solution)/shard_map/ppermute | solution.py:17
  56.7 8.6 %collective-permute-done.1 = f32[8,128,128]{2,1,0:T(8,128)S(1)} collective-permute-done((f32[8,128,128]{2,1,0:T(8,128)S(1)}, f32[8,128,128]{2,1,0:T(8,128)S(1)}, u32[]{:S(2)}, u32[]{:S(2)}) %collective-permute-start.1) | collective-permute-done | bytes 524320 | tf_op jit(solution)/shard_map/ppermute | solution.py:17
  65.3 1.2 %fusion.43 = f32[8,128,128]{2,1,0:T(8,128)S(1)} fusion(f32[8,128,128]{2,1,0:T(8,128)S(1)} %collective-permute-done.1, f32[8,128,256]{2,1,0:T(8,128)S(1)} %fusion.19), kind=kOutput, calls=%fused_computation.67 | convolution fusion | flops 201326592 | bytes 1572864 | tf_op jit(solution)/shard_map/hjd,htd->hjt/dot_general | solution.py:96
  66.5 1.6 %convolution_subtract_fusion.1 = f32[8,128,128]{2,1,0:T(8,128)} fusion(f32[8,128,128]{2,1,0:T(8,128)S(1)} %collective-permute-done.1, f32[8,128,128]{2,1,0:T(8,128)S(1)} %fusion.43, f32[128,8,128]{2,0,1:T(8,128)S(1)} %copy.23, f32[8,128]{1,0:T(8,128)S(1)} %add_sqrt_fusion), kind=kOutput, calls=%fused_computation.18 | convolution fusion | flops 201588736 | bytes 2101248 | tf_op jit(solution)/shard_map/hjt,htd->hjd/dot_general | solution.py:97
  68.1 1.9 %collective-permute-start.2 = (f32[8,128,128]{2,1,0:T(8,128)}, f32[8,128,128]{2,1,0:T(8,128)}, u32[]{:S(2)}, u32[]{:S(2)}) collective-permute-start(f32[8,128,128]{2,1,0:T(8,128)} %convolution_subtract_fusion.1), channel_id=1, source_target_pairs={{0,4},{4,8},{8,12},{12,16},{16,20},{20,24},{24,28},{28,32},{32,36}... | collective-permute-start | bytes 1572872 | tf_op jit(solution)/shard_map/ppermute | solution.py:17
  70.0 0.1 fusion.67
  70.1 1.9 %collective-permute-start.5 = (bf16[128,1024]{1,0:T(8,128)(2,1)S(1)}, bf16[128,1024]{1,0:T(8,128)(2,1)S(1)}, u32[]{:S(2)}, u32[]{:S(2)}) collective-permute-start(bf16[128,1024]{1,0:T(8,128)(2,1)S(1)} %collective-permute-done.4), channel_id=1, source_target_pairs={{0,4},{4,8},{8,12},{12,16},{16,20},{20,24},{24,28},{28,32},{32,36}... | collective-permute-start | bytes 786440 | tf_op jit(solution)/shard_map/ppermute | solution.py:17
  72.1 1.0 %convolution_subtract_fusion.4 = f32[8,128,128]{2,1,0:T(8,128)S(1)} fusion(f32[8,128,128]{1,2,0:T(8,128)S(1)} %fusion.10, f32[8,128,256]{2,1,0:T(8,128)S(1)} %fusion.19, bf16[128,1024]{1,0:T(8,128)(2,1)S(1)} %copy-done), kind=kOutput, calls=%fused_computation.21 | convolution fusion | flops 201588736 | bytes 1835008 | tf_op jit(solution)/shard_map/hit,htd->hid/dot_general | solution.py:87
  73.1 11.8 %collective-permute-done.5 = bf16[128,1024]{1,0:T(8,128)(2,1)S(1)} collective-permute-done((bf16[128,1024]{1,0:T(8,128)(2,1)S(1)}, bf16[128,1024]{1,0:T(8,128)(2,1)S(1)}, u32[]{:S(2)}, u32[]{:S(2)}) %collective-permute-start.5) | collective-permute-done | bytes 262176 | tf_op jit(solution)/shard_map/ppermute | solution.py:17
  84.9 1.1 %pad_maximum_fusion = bf16[512,1024]{1,0:T(8,128)(2,1)S(1)} fusion(bf16[128,1024]{1,0:T(8,128)(2,1)} %param.11, bf16[128,1024]{1,0:T(8,128)(2,1)} %collective-permute-done.3, bf16[128,1024]{1,0:T(8,128)(2,1)S(1)} %collective-permute-done.4, bf16[128,1024]{1,0:T(8,128)(2,1)S(1)} %collective-permute-done.5), kind=kLoop, calls=%fused_computation.39 | loop fusion | flops 4194304 | bytes 2097152 | tf_op jit(solution)/shard_map/concatenate | solution.py:144
  86.0 1.3 %copy.39 = bf16[512,1024]{0,1:T(8,128)(2,1)} copy(bf16[512,1024]{1,0:T(8,128)(2,1)S(1)} %pad_maximum_fusion) | data formatting | bytes 2097152 | tf_op jit(solution)/shard_map/concatenate | solution.py:144
  87.3 3.1 %fusion.3 = f32[8,128,384]{2,1,0:T(8,128)S(1)} fusion(f32[8,128,128]{2,1,0:T(8,128)S(1)} %convolution_subtract_fusion.4, f32[8,128,128]{2,1,0:T(8,128)S(1)} %collective-permute-done, f32[8,128,128]{2,1,0:T(8,128)S(1)} %collective-permute-done.1, f32[8,128,128]{2,1,0:T(8,128)} %collective-permute-done.2), kind=kOutput, calls=%fused_computation.10 | convolution fusion | flops 604766208 | bytes 3670016 | tf_op jit(solution)/shard_map/hid,hjd->hij/dot_general | solution.py:102
  90.4 0.4 fusion.25
  90.8 0.6 fusion.1
  91.4 0.2 copy-done.7
  91.6 0.7 fusion.16
  92.4 0.8 copy.40
  (41 shorter events, 0.5 us)
Async XLA Ops:
  0.0 43.9 %copy-start = (bf16[128,1024]{1,0:T(8,128)(2,1)S(1)}, bf16[128,1024]{1,0:T(8,128)(2,1)}, u32[]{:S(2)}) copy-start(bf16[128,1024]{1,0:T(8,128)(2,1)} %param.9) | copy-start | bytes 786436
  3.7 14.7 %copy-start.2 = (f32[8,128,128]{2,1,0:T(8,128)}, f32[8,128,128]{2,1,0:T(8,128)S(1)}, u32[]{:S(2)}) copy-start(f32[8,128,128]{2,1,0:T(8,128)S(1)} %fusion.9) | copy-start | bytes 1572868
  21.8 2.9 %copy-start.1 = (f32[8,4,32,4,32]{4,3,2,1,0:T(4,128)S(1)}, f32[8,4,32,4,32]{4,3,2,1,0:T(4,128)}, u32[]{:S(2)}) copy-start(f32[8,4,32,4,32]{4,3,2,1,0:T(4,128)} %reshape.259) | copy-start | bytes 1572868
  23.1 0.8 copy-start.5
  25.6 4.0 %copy-start.4 = (f32[8,2,64,2,64]{4,3,2,1,0:T(2,128)S(1)}, f32[8,2,64,2,64]{4,3,2,1,0:T(2,128)}, u32[]{:S(2)}) copy-start(f32[8,2,64,2,64]{4,3,2,1,0:T(2,128)} %reshape.260) | copy-start | bytes 1572868
  30.3 1.0 %copy-start.3 = (f32[8,128,128]{2,1,0:T(8,128)S(1)}, f32[8,128,128]{2,1,0:T(8,128)}, u32[]{:S(2)}) copy-start(f32[8,128,128]{2,1,0:T(8,128)} %copy-done.2) | copy-start | bytes 1572868
  31.1 1.1 %copy-start.8 = (bf16[128,1024]{1,0:T(8,128)(2,1)S(1)}, bf16[128,1024]{1,0:T(8,128)(2,1)}, u32[]{:S(2)}) copy-start(bf16[128,1024]{1,0:T(8,128)(2,1)} %param.10) | copy-start | bytes 786436
  31.8 1.5 %copy-start.6 = (f32[8,128,128]{2,1,0:T(8,128)S(1)}, f32[8,128,128]{2,1,0:T(8,128)}, u32[]{:S(2)}) copy-start(f32[8,128,128]{2,1,0:T(8,128)} %broadcast_multiply_fusion) | copy-start | bytes 1572868
  33.2 7.9 %copy-start.10 = (s32[1,3]{1,0:T(1,128)S(1)}, s32[1,3]{1,0:T(1,128)}, u32[]{:S(2)}) copy-start(s32[1,3]{1,0:T(1,128)} %param.15) | copy-start | bytes 40
  33.2 8.5 %copy-start.9 = (s32[8192]{0:T(1024)S(1)}, s32[8192]{0:T(1024)}, u32[]{:S(2)}) copy-start(s32[8192]{0:T(1024)} %param.14) | copy-start | bytes 98308
  35.7 13.8 %collective-permute-start = (f32[8,128,128]{2,1,0:T(8,128)S(1)}, f32[8,128,128]{2,1,0:T(8,128)S(1)}, u32[]{:S(2)}, u32[]{:S(2)}) collective-permute-start(f32[8,128,128]{2,1,0:T(8,128)S(1)} %convolution_subtract_fusion.3), channel_id=1, source_target_pairs={{0,4},{4,8},{8,12},{12,16},{16,20},{20,24},{24,28},{28,32},{32,36}... | collective-permute-start | bytes 1572872 | tf_op jit(solution)/shard_map/ppermute | solution.py:17
  37.6 17.1 %collective-permute-start.3 = (bf16[128,1024]{1,0:T(8,128)(2,1)}, bf16[128,1024]{1,0:T(8,128)(2,1)}, u32[]{:S(2)}, u32[]{:S(2)}) collective-permute-start(bf16[128,1024]{1,0:T(8,128)(2,1)} %param.11), channel_id=1, source_target_pairs={{0,4},{4,8},{8,12},{12,16},{16,20},{20,24},{24,28},{28,32},{32,36}... | collective-permute-start | bytes 786440 | tf_op jit(solution)/shard_map/ppermute | solution.py:17
  51.5 13.8 %collective-permute-start.1 = (f32[8,128,128]{2,1,0:T(8,128)S(1)}, f32[8,128,128]{2,1,0:T(8,128)S(1)}, u32[]{:S(2)}, u32[]{:S(2)}) collective-permute-start(f32[8,128,128]{2,1,0:T(8,128)S(1)} %convolution_subtract_fusion.2), channel_id=1, source_target_pairs={{0,4},{4,8},{8,12},{12,16},{16,20},{20,24},{24,28},{28,32},{32,36}... | collective-permute-start | bytes 1572872 | tf_op jit(solution)/shard_map/ppermute | solution.py:17
  54.7 15.4 %collective-permute-start.4 = (bf16[128,1024]{1,0:T(8,128)(2,1)}, bf16[128,1024]{1,0:T(8,128)(2,1)S(1)}, u32[]{:S(2)}, u32[]{:S(2)}) collective-permute-start(bf16[128,1024]{1,0:T(8,128)(2,1)} %collective-permute-done.3), channel_id=1, source_target_pairs={{0,4},{4,8},{8,12},{12,16},{16,20},{20,24},{24,28},{28,32},{32,36}... | collective-permute-start | bytes 786440 | tf_op jit(solution)/shard_map/ppermute | solution.py:17
  68.1 19.3 %collective-permute-start.2 = (f32[8,128,128]{2,1,0:T(8,128)}, f32[8,128,128]{2,1,0:T(8,128)}, u32[]{:S(2)}, u32[]{:S(2)}) collective-permute-start(f32[8,128,128]{2,1,0:T(8,128)} %convolution_subtract_fusion.1), channel_id=1, source_target_pairs={{0,4},{4,8},{8,12},{12,16},{16,20},{20,24},{24,28},{28,32},{32,36}... | collective-permute-start | bytes 1572872 | tf_op jit(solution)/shard_map/ppermute | solution.py:17
  70.1 14.8 %collective-permute-start.5 = (bf16[128,1024]{1,0:T(8,128)(2,1)S(1)}, bf16[128,1024]{1,0:T(8,128)(2,1)S(1)}, u32[]{:S(2)}, u32[]{:S(2)}) collective-permute-start(bf16[128,1024]{1,0:T(8,128)(2,1)S(1)} %collective-permute-done.4), channel_id=1, source_target_pairs={{0,4},{4,8},{8,12},{12,16},{16,20},{20,24},{24,28},{28,32},{32,36}... | collective-permute-start | bytes 786440 | tf_op jit(solution)/shard_map/ppermute | solution.py:17
  90.4 1.2 %copy-start.7 = (bf16[512,1024]{0,1:T(8,128)(2,1)S(1)}, bf16[512,1024]{0,1:T(8,128)(2,1)}, u32[]{:S(2)}) copy-start(bf16[512,1024]{0,1:T(8,128)(2,1)} %copy.39) | copy-start | bytes 3145732
where the time goes:
time: 93.8 us; the launch traced here: 93.2 us
  waiting for transfers between devices  25.4 us (27%)
  matrix products  24.2 us (26%)
  local copies, waits for them, and re-layouts  22.4 us (24%)
  starting transfers between devices  13.1 us (14%)
  other arithmetic  7.67 us (8%)
    ppermute x6, waiting for transfers between devices, passed_along(): return lax.ppermute(value, axis, pairs)  25.4 us
    ppermute x6, starting transfers between devices, passed_along(): return lax.ppermute(value, axis, pairs)  13.1 us
    reshape x6, local copies, waits for them, and re-layouts, diagonal_blocks(): matrix.reshape(heads, count, size, count, size)  11.8 us
    dot_general x12, matrix products, paired_product(): return jnp.einsum('hpab,hpbc->hpac', left, right, precision=HIGHEST)  8.19 us
    gather x3, local copies, waits for them, and re-layouts, diagonal_blocks(): jnp.diagonal(matrix.reshape(heads, count, size, count, size), axis1=1, ax...  3.94 us
    dot_general x1, matrix products, weights_of(): jnp.einsum('hid,hjd->hij', turned, far_keys, precision=HIGHEST)  3.06 us
    dot_general x2, matrix products, advance(): inner = jnp.einsum('hjd,htd->hjt', carried, back_rows, precision=HIGHEST)  2.42 us
    unnamed x24, local copies, waits for them, and re-layouts  2.41 us
  transfers between devices with their start and end apart: 6, of which 3 were waited for; matrix products, arithmetic and copies ran while one was open for 14% of the time, Pallas kernels for 0%

commit v1 on v0

v1 whole, which is shorter than its diff:
```python
import jax
import jax.numpy as jnp
from jax import lax
from jax.experimental import pallas as pl
from jax.experimental.pallas import tpu as pltpu
from jax.sharding import PartitionSpec as P

HEAD_DIM = 128
BACK = 3
EPSILON = 1e-06
F32 = jnp.float32
BF16 = jnp.bfloat16
VMEM_LIMIT = 48 << 20


def dot_nn(left, right):
    return lax.dot_general(left, right, (((1,), (0,)), ((), ())), preferred_element_type=F32)


def dot_nt(left, right):
    return lax.dot_general(left, right, (((1,), (1,)), ((), ())), preferred_element_type=F32)


def columns(head):
    return slice(head * HEAD_DIM, (head + 1) * HEAD_DIM)


def upper_inverse(strict_uppers, row, col):
    size = row.shape[0]
    eye = jnp.where(row == col, 1.0, 0.0).astype(F32)
    base = 16
    same = (row // base) == (col // base)
    diag = [jnp.where(same, u, 0.0) for u in strict_uppers]
    power = [d.astype(BF16) for d in diag]
    inverse = [eye - d for d in diag]
    reach = 2
    while reach < base:
        power = [dot_nn(p, p).astype(BF16) for p in power]
        inverse = [x + dot_nn(x.astype(BF16), p) for x, p in zip(inverse, power)]
        reach *= 2
    span = 2 * base
    while span <= size:
        joined = ((row // span) == (col // span)) & ((row // (span // 2)) != (col // (span // 2)))
        corner = [jnp.where(joined, u, 0.0).astype(BF16) for u in strict_uppers]
        half = [x.astype(BF16) for x in inverse]
        mid = [dot_nn(x, e).astype(BF16) for x, e in zip(half, corner)]
        inverse = [x - dot_nn(m, y) for x, m, y in zip(inverse, mid, half)]
        span *= 2
    return inverse


def prep_kernel(k_ref, w_ref, beta_ref, wb_ref, bt_ref, cct_ref, c_ref, d_ref):
    heads = beta_ref.shape[1]
    length = k_ref.shape[0]
    row = lax.broadcasted_iota(jnp.int32, (length, length), 0)
    col = lax.broadcasted_iota(jnp.int32, (length, length), 1)
    upper = row < col
    units, turned_units, uppers, rights = [], [], [], []
    for h in range(heads):
        w = w_ref[:, columns(h)].astype(F32)
        scale = lax.rsqrt(jnp.sum(w * w, axis=-1, keepdims=True) + EPSILON)
        unit = w * scale
        wb = unit.astype(BF16)
        bw = unit * beta_ref[:, h : h + 1].astype(F32)
        units.append(wb)
        turned_units.append(jnp.transpose(bw).astype(BF16))
        wb_ref[:, columns(h)] = wb
        both = dot_nt(jnp.concatenate([wb, k_ref[:, columns(h)]], axis=0), bw.astype(BF16))
        uppers.append(jnp.where(upper, both[:length], 0.0))
        rights.append(jnp.where(upper, both[length:], 0.0).astype(BF16))
    inverse = upper_inverse(uppers, row, col)
    for h in range(heads):
        solved = dot_nn(
            jnp.concatenate([turned_units[h], rights[h]], axis=0), inverse[h].astype(BF16)
        ).astype(BF16)
        bt_ref[:, columns(h)] = solved[:length]
        cct_ref[:, columns(h)] = solved[length:]
        moved = dot_nn(solved, units[h])
        d_ref[:, columns(h)] = moved[:length].astype(BF16)
        c_ref[:, columns(h)] = (k_ref[:, columns(h)].astype(F32) - moved[length:]).astype(BF16)


def query_kernel(q_ref, k_ref, wb_ref, bt_ref, cct_ref, t_ref, own_ref):
    length = q_ref.shape[0]
    row = lax.broadcasted_iota(jnp.int32, (length, length), 0)
    col = lax.broadcasted_iota(jnp.int32, (length, length), 1)
    for h in range(q_ref.shape[1] // HEAD_DIM):
        q = q_ref[:, columns(h)]
        both = dot_nt(q, jnp.concatenate([wb_ref[:, columns(h)], k_ref[:, columns(h)]], axis=0))
        query_w = jnp.where(col <= row, both[:, :length], 0.0).astype(BF16)
        turn = dot_nt(
            query_w, jnp.concatenate([bt_ref[:, columns(h)], cct_ref[:, columns(h)]], axis=0)
        )
        t_ref[:, columns(h)] = (q.astype(F32) - turn[:, :length]).astype(BF16)
        own_ref[:, columns(h)] = both[:, length:] - turn[:, length:]


def pair_kernel(c_ref, d_ref, other_ref, x2_ref, e_ref):
    length = c_ref.shape[0]
    for h in range(c_ref.shape[1] // HEAD_DIM):
        c, d, o = c_ref[:, columns(h)], d_ref[:, columns(h)], other_ref[:, columns(h)]
        both = dot_nn(jnp.concatenate([c, d], axis=0), o)
        x2_ref[:, columns(h)] = (c.astype(F32) - both[:length]).astype(BF16)
        e_ref[:, columns(h)] = (d.astype(F32) + o.astype(F32) - both[length:]).astype(BF16)


def third_kernel(x1_ref, e_ref, x3_ref):
    for h in range(x1_ref.shape[1] // HEAD_DIM):
        x = x1_ref[:, columns(h)]
        x3_ref[:, columns(h)] = (x.astype(F32) - dot_nn(x, e_ref[:, columns(h)])).astype(BF16)


def final_kernel(
    visits_ref, seg_ref, t_ref, other_ref, own_ref, v_ref, near_k_ref, near_v_ref,
    even_k2, even_v2, even_k3, even_v3, odd_k2, odd_v2, odd_k3, odd_v3,
    out_ref, k2, v2, k3, v3, t2, sems,
):
    length = t_ref.shape[0]
    block = lax.axis_index("seq")
    odd = lax.rem(block, 2)
    targets = (k2, v2, k3, v3)

    @pl.when(odd == 0)
    def _():
        for i, (src, dst) in enumerate(zip((even_k2, even_v2, even_k3, even_v3), targets)):
            pltpu.make_async_copy(src, dst, sems.at[i]).start()
        t2[...] = t_ref[...]

    @pl.when(odd == 1)
    def _():
        for i, (src, dst) in enumerate(zip((odd_k2, odd_v2, odd_k3, odd_v3), targets)):
            pltpu.make_async_copy(src, dst, sems.at[i]).start()
        for h in range(t_ref.shape[1] // HEAD_DIM):
            t = t_ref[:, columns(h)]
            t2[:, columns(h)] = (t.astype(F32) - dot_nt(t, other_ref[:, columns(h)])).astype(BF16)

    row = lax.broadcasted_iota(jnp.int32, (length, length), 0)
    col = lax.broadcasted_iota(jnp.int32, (length, length), 1)

    def seg_row(r):
        at = jnp.maximum(block - r, 0)
        return seg_ref[pl.ds(at, 1), :].astype(F32)

    seg_q = jnp.transpose(jnp.broadcast_to(seg_row(0), (length, length)))
    allowed = []
    for r in (3, 2, 1):
        open_ = jnp.where(block - r >= 0, visits_ref[0, r - 1], 0)
        allowed.append((seg_q == seg_row(r)) & (open_ > 0))
    allowed.append((seg_q == seg_row(0)) & (col <= row))
    allow = jnp.concatenate([jnp.where(a, 0.0, -1e30) for a in allowed], axis=1)
    for i, dst in enumerate(targets):
        pltpu.make_async_copy(dst, dst, sems.at[i]).wait()
    for h in range(t_ref.shape[1] // HEAD_DIM):
        c = columns(h)
        far = dot_nt(t2[:, c], jnp.concatenate([k3[:, c], k2[:, c]], axis=0))
        near = dot_nt(t_ref[:, c], near_k_ref[:, c])
        scores = jnp.concatenate([far, near, own_ref[:, c]], axis=1) * HEAD_DIM**-0.5 + allow
        top = jnp.max(scores, axis=-1, keepdims=True)
        weights = jnp.exp(scores - top)
        total = jnp.sum(weights, axis=-1, keepdims=True)
        rows = jnp.concatenate([v3[:, c], v2[:, c], near_v_ref[:, c], v_ref[:, c]], axis=0)
        out_ref[:, c] = (dot_nn(weights.astype(BF16), rows) / total).astype(BF16)


def call(body, outs, *args, scratch=(), specs=None, flops=0, name=None):
    size = sum(a.size * a.dtype.itemsize for a in args) + sum(o.size * o.dtype.itemsize for o in outs)
    vmem = pl.BlockSpec(memory_space=pltpu.VMEM)
    return pl.pallas_call(
        body,
        out_shape=outs,
        in_specs=specs or [vmem] * len(args),
        out_specs=[vmem] * len(outs),
        scratch_shapes=scratch,
        compiler_params=pltpu.CompilerParams(vmem_limit_bytes=VMEM_LIMIT),
        cost_estimate=pl.CostEstimate(flops=flops, bytes_accessed=size, transcendentals=0),
        name=name,
    )(*args)


def shards(queries, keys, values, transitions, betas, segments, visits):
    shape = jax.ShapeDtypeStruct(queries.shape, BF16)
    wide = jax.ShapeDtypeStruct(queries.shape, F32)
    size = lax.axis_size("seq")
    next_one = [(i, i + 1) for i in range(size - 1)]
    swap = [(i, i ^ 1) for i in range(size)]
    next_even = [(i, i + 2) for i in range(0, size - 2, 2)]
    to_odd = [(i, i + 1) for i in range(0, size, 2)]

    near_v = lax.ppermute(values, "seq", next_one)
    unit, back_t, coef_t, carried, op = call(
        prep_kernel, [shape] * 5, keys, transitions, betas, name="prep"
    )
    near_k = lax.ppermute(carried, "seq", next_one)
    other = lax.ppermute(op, "seq", swap)
    turned, own = call(
        query_kernel, [shape, wide], queries, keys, unit, back_t, coef_t, name="query"
    )
    far2, both = call(pair_kernel, [shape] * 2, carried, op, other, name="pair")
    even_v2 = lax.ppermute(values, "seq", next_even)
    even_k2 = lax.ppermute(far2, "seq", next_even)
    (far3,) = call(third_kernel, [shape], near_k, both, name="third")
    even_k3 = lax.ppermute(far3, "seq", next_even)
    even_v3 = lax.ppermute(near_v, "seq", next_even)
    odd_k2 = lax.ppermute(near_k, "seq", to_odd)
    odd_v2 = lax.ppermute(near_v, "seq", to_odd)
    odd_k3 = lax.ppermute(even_k2, "seq", to_odd)
    odd_v3 = lax.ppermute(even_v2, "seq", to_odd)
    vmem = pl.BlockSpec(memory_space=pltpu.VMEM)
    smem = pl.BlockSpec(memory_space=pltpu.SMEM)
    hbm = pl.BlockSpec(memory_space=pl.ANY)
    (out,) = call(
        final_kernel,
        [shape],
        visits,
        segments.reshape(size, -1),
        turned,
        other,
        own,
        values,
        near_k,
        near_v,
        even_k2,
        even_v2,
        even_k3,
        even_v3,
        odd_k2,
        odd_v2,
        odd_k3,
        odd_v3,
        specs=[smem] + [vmem] * 7 + [hbm] * 8,
        scratch=[pltpu.VMEM(queries.shape, BF16)] * 5 + [pltpu.SemaphoreType.DMA((4,))],
        name="final",
    )
    return out


def solution(mesh):
    return jax.shard_map(
        shards,
        mesh=mesh,
        in_specs=(
            P("seq", "head"),
            P("seq", "head"),
            P("seq", "head"),
            P("seq", "head"),
            P("seq", "head"),
            P(),
            P("seq", None),
        ),
        out_specs=P("seq", "head"),
        check_vma=False,
    )
```

time: 93.8 us -> 39.6 us (0.42)
  matrix products: 24.2 us -> 0 us
  waiting for transfers between devices: 25.4 us -> 5.81 us
  local copies, waits for them, and re-layouts: 22.4 us -> 3.36 us
  starting transfers between devices: 13.1 us -> 22.4 us
  other arithmetic: 7.67 us -> 0 us
  Pallas kernels: 0 us -> 7.39 us
    dot_general x26 -> x0, matrix products: 24.2 us -> none  [the longest x12 8.19 us: paired_product(): return jnp.einsum('hpab,hpbc->hpac', left, right, precision=HIGHEST)]
    ppermute x6 -> x11, waiting for transfers between devices: 25.4 us -> 5.81 us  [the longest x1 4.67 us: shards(): even_v3 = lax.ppermute(near_v, 'seq', next_even)]
    reshape x7 -> x0, local copies, waits for them, and re-layouts: 12 us -> none  [the longest x6 11.8 us: diagonal_blocks(): matrix.reshape(heads, count, size, count, size)]
    ppermute x6 -> x11, starting transfers between devices: 13.1 us -> 22.4 us  [the longest x1 3.4 us: shards(): even_v2 = lax.ppermute(values, 'seq', next_even)]
    pallas_call x0 -> x5, Pallas kernels: none -> 7.39 us  [call(): pl.pallas_call(body, out_shape=outs, in_specs=specs or [vmem] * len(args)...]
    gather x4 -> x0, local copies, waits for them, and re-layouts: 4.55 us -> none  [the longest x3 3.94 us: diagonal_blocks(): jnp.diagonal(matrix.reshape(heads, count, size, count, size), axis1=1, ax...]
    concatenate x6 -> x0, other arithmetic: 2.43 us -> none  [the longest x2 1.31 us: unit_inverse(): inverse = jnp.concatenate([upper, bottom], axis=-2)]
    gather x1 -> x0, other arithmetic: 1.97 us -> none  [weights_of(): visited = jnp.repeat(visited, length, total_repeat_length=spread)]
  transfers between devices with their start and end apart: 6 -> 11, of which waited for: 3 -> 2; matrix products, arithmetic and copies ran while one was open for 14% -> 2% of each run, Pallas kernels for 0% -> 9%
where the time goes in v1:
time: 39.6 us; the launch traced here: 39.2 us
  starting transfers between devices  22.4 us (57%)
  Pallas kernels  7.39 us (19%)
  waiting for transfers between devices  5.81 us (15%)
  local copies, waits for them, and re-layouts  3.36 us (8%)
    pallas_call x5, Pallas kernels, call(): pl.pallas_call(body, out_shape=outs, in_specs=specs or [vmem] * len(args)...  7.39 us
    ppermute x1, waiting for transfers between devices, shards(): even_v3 = lax.ppermute(near_v, 'seq', next_even)  4.67 us
    ppermute x1, starting transfers between devices, shards(): even_v2 = lax.ppermute(values, 'seq', next_even)  3.4 us
    unnamed x15, local copies, waits for them, and re-layouts  3.36 us
    ppermute x1, starting transfers between devices, shards(): even_v3 = lax.ppermute(near_v, 'seq', next_even)  3.23 us
    ppermute x1, starting transfers between devices, shards(): even_k2 = lax.ppermute(far2, 'seq', next_even)  3.11 us
    ppermute x1, starting transfers between devices, shards(): near_k = lax.ppermute(carried, 'seq', next_one)  1.92 us
    ppermute x1, starting transfers between devices, shards(): even_k3 = lax.ppermute(far3, 'seq', next_even)  1.92 us
  transfers between devices with their start and end apart: 11, of which 2 were waited for; matrix products, arithmetic and copies ran while one was open for 2% of the time, Pallas kernels for 9%

profile of v1, /device:TPU:136, one launch (start us, length us, event | category | flops | bytes accessed | tf_op | source)
XLA Modules:
  0.0 39.2 jit_solution(12738203027974764049)
XLA Ops:
  0.0 1.9 %collective-permute-start.2 = (bf16[128,1024]{1,0:T(8,128)(2,1)}, bf16[128,1024]{1,0:T(8,128)(2,1)S(1)}, u32[]{:S(2)}, u32[]{:S(2)}) collective-permute-start(bf16[128,1024]{1,0:T(8,128)(2,1)} %v_ref.1), channel_id=1, source_target_pairs={{0,4},{4,8},{8,12},{12,16},{16,20},{20,24},{24,28},{28,32},{32,36}... | collective-permute-start | bytes 786440 | tf_op jit(solution)/shard_map/ppermute | solution.py:189
  1.9 0.8 %copy.8.beta_ref = bf16[128,8]{1,0:T(8,128)(2,1)S(1)} copy(bf16[128,8]{0,1:T(8,128)(2,1)} %param.11) | data formatting | bytes 4096 | tf_op args[4]
  2.7 0.0 copy-start
  2.7 0.9 %copy-done = bf16[128,1024]{1,0:T(8,128)(2,1)S(1)} copy-done((bf16[128,1024]{1,0:T(8,128)(2,1)S(1)}, bf16[128,1024]{1,0:T(8,128)(2,1)}, u32[]{:S(2)}) %copy-start) | copy-done | bytes 262168
  3.7 0.0 copy-start.4
  3.7 0.9 %copy-done.4 = bf16[128,1024]{1,0:T(8,128)(2,1)S(1)} copy-done((bf16[128,1024]{1,0:T(8,128)(2,1)S(1)}, bf16[128,1024]{1,0:T(8,128)(2,1)}, u32[]{:S(2)}) %copy-start.4) | copy-done | bytes 262168
  4.6 0.0 copy-start.3
  4.6 2.5 %prep.1 = (bf16[128,1024]{1,0:T(8,128)(2,1)S(1)}, bf16[128,1024]{1,0:T(8,128)(2,1)S(1)}, bf16[128,1024]{1,0:T(8,128)(2,1)S(1)}, bf16[128,1024]{1,0:T(8,128)(2,1)S(1)}, bf16[128,1024]{1,0:T(8,128)(2,1)S(1)}) custom-call(bf16[128,1024]{1,0:T(8,128)(2,1)S(1)} %copy-done, bf16[128,1024]{1,0:T(8,128)(2,1)S(1)} %copy-done.4, bf16[128,8]{1,0:T(8,128)(2,1)S(1)} %copy.8.beta_ref), custom_call_target="tpu_custom_call" | custom-call | bytes 1837056 | tf_op jit(solution)/shard_map/prep/pallas_call | solution.py:168
  7.2 1.7 %collective-permute-start = (bf16[128,1024]{1,0:T(8,128)(2,1)S(1)}, bf16[128,1024]{1,0:T(8,128)(2,1)S(1)}, u32[]{:S(2)}, u32[]{:S(2)}) collective-permute-start(bf16[128,1024]{1,0:T(8,128)(2,1)S(1)} %get-tuple-element.18.d_ref), channel_id=1, source_target_pairs={{0,4},{4,0},{8,12},{12,8},{16,20},{20,16},{24,28},{28,24},{32,36},... | collective-permute-start | bytes 786440 | tf_op jit(solution)/shard_map/ppermute | solution.py:194
  8.9 1.9 %collective-permute-start.1 = (bf16[128,1024]{1,0:T(8,128)(2,1)S(1)}, bf16[128,1024]{1,0:T(8,128)(2,1)S(1)}, u32[]{:S(2)}, u32[]{:S(2)}) collective-permute-start(bf16[128,1024]{1,0:T(8,128)(2,1)S(1)} %get-tuple-element.20.c_ref), channel_id=1, source_target_pairs={{0,4},{4,8},{8,12},{12,16},{16,20},{20,24},{24,28},{28,32},{32,36}... | collective-permute-start | bytes 786440 | tf_op jit(solution)/shard_map/ppermute | solution.py:193
  10.8 0.0 copy-done.3
  10.8 3.4 %collective-permute-start.4 = (bf16[128,1024]{1,0:T(8,128)(2,1)S(1)}, bf16[128,1024]{1,0:T(8,128)(2,1)S(1)}, u32[]{:S(2)}, u32[]{:S(2)}) collective-permute-start(bf16[128,1024]{1,0:T(8,128)(2,1)S(1)} %copy-done.3), channel_id=1, source_target_pairs={{0,8},{8,16},{16,24},{24,32},{32,40},{40,48},{48,56},{56,64},{64,7... | collective-permute-start | bytes 786440 | tf_op jit(solution)/shard_map/ppermute | solution.py:199
  14.2 0.0 collective-permute-done.2.near_v_ref
  14.2 1.3 %collective-permute-start.8 = (bf16[128,1024]{1,0:T(8,128)(2,1)S(1)}, bf16[128,1024]{1,0:T(8,128)(2,1)S(1)}, u32[]{:S(2)}, u32[]{:S(2)}) collective-permute-start(bf16[128,1024]{1,0:T(8,128)(2,1)S(1)} %collective-permute-done.2.near_v_ref), channel_id=1, source_target_pairs={{0,4},{8,12},{16,20},{24,28},{32,36},{40,44},{48,52},{56,60},{64,6... | collective-permute-start | bytes 786440 | tf_op jit(solution)/shard_map/ppermute | solution.py:205
  15.5 0.0 collective-permute-done.other_ref
  15.5 0.3 pair.1
  15.8 3.1 %collective-permute-start.3 = (bf16[128,1024]{1,0:T(8,128)(2,1)S(1)}, bf16[128,1024]{1,0:T(8,128)(2,1)S(1)}, u32[]{:S(2)}, u32[]{:S(2)}) collective-permute-start(bf16[128,1024]{1,0:T(8,128)(2,1)S(1)} %get-tuple-element.21), channel_id=1, source_target_pairs={{0,8},{8,16},{16,24},{24,32},{32,40},{40,48},{48,56},{56,64},{64,7... | collective-permute-start | bytes 786440 | tf_op jit(solution)/shard_map/ppermute | solution.py:200
  19.0 1.1 %collective-permute-done.1.x1_ref.near_k_ref = bf16[128,1024]{1,0:T(8,128)(2,1)S(1)} collective-permute-done((bf16[128,1024]{1,0:T(8,128)(2,1)S(1)}, bf16[128,1024]{1,0:T(8,128)(2,1)S(1)}, u32[]{:S(2)}, u32[]{:S(2)}) %collective-permute-start.1) | collective-permute-done | bytes 262176 | tf_op jit(solution)/shard_map/ppermute | solution.py:193
  20.1 0.0 copy-start.1
  20.1 0.0 copy-start.2
  20.1 0.2 third.1
  20.3 1.9 %collective-permute-start.5 = (bf16[128,1024]{1,0:T(8,128)(2,1)S(1)}, bf16[128,1024]{1,0:T(8,128)(2,1)S(1)}, u32[]{:S(2)}, u32[]{:S(2)}) collective-permute-start(bf16[128,1024]{1,0:T(8,128)(2,1)S(1)} %third.1), channel_id=1, source_target_pairs={{0,8},{8,16},{16,24},{24,32},{32,40},{40,48},{48,56},{56,64},{64,7... | collective-permute-start | bytes 786440 | tf_op jit(solution)/shard_map/ppermute | solution.py:202
  22.2 3.2 %collective-permute-start.6 = (bf16[128,1024]{1,0:T(8,128)(2,1)S(1)}, bf16[128,1024]{1,0:T(8,128)(2,1)S(1)}, u32[]{:S(2)}, u32[]{:S(2)}) collective-permute-start(bf16[128,1024]{1,0:T(8,128)(2,1)S(1)} %collective-permute-done.2.near_v_ref), channel_id=1, source_target_pairs={{0,8},{8,16},{16,24},{24,32},{32,40},{40,48},{48,56},{56,64},{64,7... | collective-permute-start | bytes 786440 | tf_op jit(solution)/shard_map/ppermute | solution.py:203
  25.5 0.0 collective-permute-done.4.even_v2
  25.5 1.3 %collective-permute-start.10 = (bf16[128,1024]{1,0:T(8,128)(2,1)S(1)}, bf16[128,1024]{1,0:T(8,128)(2,1)S(1)}, u32[]{:S(2)}, u32[]{:S(2)}) collective-permute-start(bf16[128,1024]{1,0:T(8,128)(2,1)S(1)} %collective-permute-done.4.even_v2), channel_id=1, source_target_pairs={{0,4},{8,12},{16,20},{24,28},{32,36},{40,44},{48,52},{56,60},{64,6... | collective-permute-start | bytes 786440 | tf_op jit(solution)/shard_map/ppermute | solution.py:207
  26.8 0.0 collective-permute-done.8.odd_v2
  26.8 1.3 %collective-permute-start.7 = (bf16[128,1024]{1,0:T(8,128)(2,1)S(1)}, bf16[128,1024]{1,0:T(8,128)(2,1)S(1)}, u32[]{:S(2)}, u32[]{:S(2)}) collective-permute-start(bf16[128,1024]{1,0:T(8,128)(2,1)S(1)} %collective-permute-done.1.x1_ref.near_k_ref), channel_id=1, source_target_pairs={{0,4},{8,12},{16,20},{24,28},{32,36},{40,44},{48,52},{56,60},{64,6... | collective-permute-start | bytes 786440 | tf_op jit(solution)/shard_map/ppermute | solution.py:204
  28.1 0.0 collective-permute-done.3.even_k2
  28.1 1.3 %collective-permute-start.9 = (bf16[128,1024]{1,0:T(8,128)(2,1)S(1)}, bf16[128,1024]{1,0:T(8,128)(2,1)S(1)}, u32[]{:S(2)}, u32[]{:S(2)}) collective-permute-start(bf16[128,1024]{1,0:T(8,128)(2,1)S(1)} %collective-permute-done.3.even_k2), channel_id=1, source_target_pairs={{0,4},{8,12},{16,20},{24,28},{32,36},{40,44},{48,52},{56,60},{64,6... | collective-permute-start | bytes 786440 | tf_op jit(solution)/shard_map/ppermute | solution.py:206
  29.4 0.0 copy-done.1
  29.5 0.0 copy-done.2
  29.5 0.0 copy-start.5
  29.5 0.5 %query.1 = (bf16[128,1024]{1,0:T(8,128)(2,1)S(1)}, f32[128,1024]{1,0:T(8,128)S(1)}) custom-call(bf16[128,1024]{1,0:T(8,128)(2,1)S(1)} %copy-done.2, bf16[128,1024]{1,0:T(8,128)(2,1)S(1)} %copy-done.1, bf16[128,1024]{1,0:T(8,128)(2,1)S(1)} %get-tuple-element.14.wb_ref, bf16[128,1024]{1,0:T(8,128)(2,1)S(1)} %get-tuple-element.15.bt_ref, ...), custom_call_target="tpu_custom_call" | custom-call | bytes 2097152 | tf_op jit(solution)/shard_map/query/pallas_call | solution.py:168
  30.0 4.7 %collective-permute-done.6.even_v3 = bf16[128,1024]{1,0:T(8,128)(2,1)S(1)} collective-permute-done((bf16[128,1024]{1,0:T(8,128)(2,1)S(1)}, bf16[128,1024]{1,0:T(8,128)(2,1)S(1)}, u32[]{:S(2)}, u32[]{:S(2)}) %collective-permute-start.6) | collective-permute-done | bytes 262176 | tf_op jit(solution)/shard_map/ppermute | solution.py:203
  34.7 0.0 collective-permute-done.10.odd_v3
  34.7 0.0 collective-permute-done.5.even_k3
  34.7 0.0 collective-permute-done.7.odd_k2
  34.7 0.0 collective-permute-done.9.odd_k3
  34.7 0.0 copy-start.6
  34.7 0.0 copy-done.5
  34.8 0.6 %copy-done.6 = s32[1,3]{1,0:T(1,128)S(1)} copy-done((s32[1,3]{1,0:T(1,128)S(1)}, s32[1,3]{1,0:T(1,128)}, u32[]{:S(2)}) %copy-start.6) | copy-done | bytes 36
  35.4 3.8 %final.1 = bf16[128,1024]{1,0:T(8,128)(2,1)} custom-call(s32[1,3]{1,0:T(1,128)S(1)} %copy-done.6, s32[64,128]{1,0:T(8,128)S(1)} %bitcast.1, bf16[128,1024]{1,0:T(8,128)(2,1)S(1)} %get-tuple-element.17.t_ref, bf16[128,1024]{1,0:T(8,128)(2,1)S(1)} %collective-permute-done.other_ref, f32[128,1024]{1,0:T(8,128)S(1)} %get-tuple-element.19.own_ref, ...), custom_call_target="tpu_custom_call" | custom-call | bytes 4227084 | tf_op jit(solution)/shard_map/final/pallas_call | solution.py:168
Async XLA Ops:
  0.0 14.2 %collective-permute-start.2 = (bf16[128,1024]{1,0:T(8,128)(2,1)}, bf16[128,1024]{1,0:T(8,128)(2,1)S(1)}, u32[]{:S(2)}, u32[]{:S(2)}) collective-permute-start(bf16[128,1024]{1,0:T(8,128)(2,1)} %v_ref.1), channel_id=1, source_target_pairs={{0,4},{4,8},{8,12},{12,16},{16,20},{20,24},{24,28},{28,32},{32,36}... | collective-permute-start | bytes 786440 | tf_op jit(solution)/shard_map/ppermute | solution.py:189
  2.7 1.0 %copy-start = (bf16[128,1024]{1,0:T(8,128)(2,1)S(1)}, bf16[128,1024]{1,0:T(8,128)(2,1)}, u32[]{:S(2)}) copy-start(bf16[128,1024]{1,0:T(8,128)(2,1)} %k_ref.3) | copy-start | bytes 786436
  3.7 0.9 %copy-start.4 = (bf16[128,1024]{1,0:T(8,128)(2,1)S(1)}, bf16[128,1024]{1,0:T(8,128)(2,1)}, u32[]{:S(2)}) copy-start(bf16[128,1024]{1,0:T(8,128)(2,1)} %w_ref.1) | copy-start | bytes 786436
  4.6 6.2 %copy-start.3 = (bf16[128,1024]{1,0:T(8,128)(2,1)S(1)}, bf16[128,1024]{1,0:T(8,128)(2,1)}, u32[]{:S(2)}) copy-start(bf16[128,1024]{1,0:T(8,128)(2,1)} %v_ref.1) | copy-start | bytes 786436
  7.2 8.4 %collective-permute-start = (bf16[128,1024]{1,0:T(8,128)(2,1)S(1)}, bf16[128,1024]{1,0:T(8,128)(2,1)S(1)}, u32[]{:S(2)}, u32[]{:S(2)}) collective-permute-start(bf16[128,1024]{1,0:T(8,128)(2,1)S(1)} %get-tuple-element.18.d_ref), channel_id=1, source_target_pairs={{0,4},{4,0},{8,12},{12,8},{16,20},{20,16},{24,28},{28,24},{32,36},... | collective-permute-start | bytes 786440 | tf_op jit(solution)/shard_map/ppermute | solution.py:194
  8.9 11.2 %collective-permute-start.1 = (bf16[128,1024]{1,0:T(8,128)(2,1)S(1)}, bf16[128,1024]{1,0:T(8,128)(2,1)S(1)}, u32[]{:S(2)}, u32[]{:S(2)}) collective-permute-start(bf16[128,1024]{1,0:T(8,128)(2,1)S(1)} %get-tuple-element.20.c_ref), channel_id=1, source_target_pairs={{0,4},{4,8},{8,12},{12,16},{16,20},{20,24},{24,28},{28,32},{32,36}... | collective-permute-start | bytes 786440 | tf_op jit(solution)/shard_map/ppermute | solution.py:193
  10.8 14.7 %collective-permute-start.4 = (bf16[128,1024]{1,0:T(8,128)(2,1)S(1)}, bf16[128,1024]{1,0:T(8,128)(2,1)S(1)}, u32[]{:S(2)}, u32[]{:S(2)}) collective-permute-start(bf16[128,1024]{1,0:T(8,128)(2,1)S(1)} %copy-done.3), channel_id=1, source_target_pairs={{0,8},{8,16},{16,24},{24,32},{32,40},{40,48},{48,56},{56,64},{64,7... | collective-permute-start | bytes 786440 | tf_op jit(solution)/shard_map/ppermute | solution.py:199
  14.2 12.6 %collective-permute-start.8 = (bf16[128,1024]{1,0:T(8,128)(2,1)S(1)}, bf16[128,1024]{1,0:T(8,128)(2,1)S(1)}, u32[]{:S(2)}, u32[]{:S(2)}) collective-permute-start(bf16[128,1024]{1,0:T(8,128)(2,1)S(1)} %collective-permute-done.2.near_v_ref), channel_id=1, source_target_pairs={{0,4},{8,12},{16,20},{24,28},{32,36},{40,44},{48,52},{56,60},{64,6... | collective-permute-start | bytes 786440 | tf_op jit(solution)/shard_map/ppermute | solution.py:205
  15.8 12.3 %collective-permute-start.3 = (bf16[128,1024]{1,0:T(8,128)(2,1)S(1)}, bf16[128,1024]{1,0:T(8,128)(2,1)S(1)}, u32[]{:S(2)}, u32[]{:S(2)}) collective-permute-start(bf16[128,1024]{1,0:T(8,128)(2,1)S(1)} %get-tuple-element.21), channel_id=1, source_target_pairs={{0,8},{8,16},{16,24},{24,32},{32,40},{40,48},{48,56},{56,64},{64,7... | collective-permute-start | bytes 786440 | tf_op jit(solution)/shard_map/ppermute | solution.py:200
  20.1 9.4 %copy-start.1 = (bf16[128,1024]{1,0:T(8,128)(2,1)S(1)}, bf16[128,1024]{1,0:T(8,128)(2,1)}, u32[]{:S(2)}) copy-start(bf16[128,1024]{1,0:T(8,128)(2,1)} %k_ref.3) | copy-start | bytes 786436
  20.1 9.4 %copy-start.2 = (bf16[128,1024]{1,0:T(8,128)(2,1)S(1)}, bf16[128,1024]{1,0:T(8,128)(2,1)}, u32[]{:S(2)}) copy-start(bf16[128,1024]{1,0:T(8,128)(2,1)} %q_ref.1) | copy-start | bytes 786436
  20.3 14.4 %collective-permute-start.5 = (bf16[128,1024]{1,0:T(8,128)(2,1)S(1)}, bf16[128,1024]{1,0:T(8,128)(2,1)S(1)}, u32[]{:S(2)}, u32[]{:S(2)}) collective-permute-start(bf16[128,1024]{1,0:T(8,128)(2,1)S(1)} %third.1), channel_id=1, source_target_pairs={{0,8},{8,16},{16,24},{24,32},{32,40},{40,48},{48,56},{56,64},{64,7... | collective-permute-start | bytes 786440 | tf_op jit(solution)/shard_map/ppermute | solution.py:202
  22.2 12.5 %collective-permute-start.6 = (bf16[128,1024]{1,0:T(8,128)(2,1)S(1)}, bf16[128,1024]{1,0:T(8,128)(2,1)S(1)}, u32[]{:S(2)}, u32[]{:S(2)}) collective-permute-start(bf16[128,1024]{1,0:T(8,128)(2,1)S(1)} %collective-permute-done.2.near_v_ref), channel_id=1, source_target_pairs={{0,8},{8,16},{16,24},{24,32},{32,40},{40,48},{48,56},{56,64},{64,7... | collective-permute-start | bytes 786440 | tf_op jit(solution)/shard_map/ppermute | solution.py:203
  25.5 9.2 %collective-permute-start.10 = (bf16[128,1024]{1,0:T(8,128)(2,1)S(1)}, bf16[128,1024]{1,0:T(8,128)(2,1)S(1)}, u32[]{:S(2)}, u32[]{:S(2)}) collective-permute-start(bf16[128,1024]{1,0:T(8,128)(2,1)S(1)} %collective-permute-done.4.even_v2), channel_id=1, source_target_pairs={{0,4},{8,12},{16,20},{24,28},{32,36},{40,44},{48,52},{56,60},{64,6... | collective-permute-start | bytes 786440 | tf_op jit(solution)/shard_map/ppermute | solution.py:207
  26.8 7.9 %collective-permute-start.7 = (bf16[128,1024]{1,0:T(8,128)(2,1)S(1)}, bf16[128,1024]{1,0:T(8,128)(2,1)S(1)}, u32[]{:S(2)}, u32[]{:S(2)}) collective-permute-start(bf16[128,1024]{1,0:T(8,128)(2,1)S(1)} %collective-permute-done.1.x1_ref.near_k_ref), channel_id=1, source_target_pairs={{0,4},{8,12},{16,20},{24,28},{32,36},{40,44},{48,52},{56,60},{64,6... | collective-permute-start | bytes 786440 | tf_op jit(solution)/shard_map/ppermute | solution.py:204
  28.1 6.6 %collective-permute-start.9 = (bf16[128,1024]{1,0:T(8,128)(2,1)S(1)}, bf16[128,1024]{1,0:T(8,128)(2,1)S(1)}, u32[]{:S(2)}, u32[]{:S(2)}) collective-permute-start(bf16[128,1024]{1,0:T(8,128)(2,1)S(1)} %collective-permute-done.3.even_k2), channel_id=1, source_target_pairs={{0,4},{8,12},{16,20},{24,28},{32,36},{40,44},{48,52},{56,60},{64,6... | collective-permute-start | bytes 786440 | tf_op jit(solution)/shard_map/ppermute | solution.py:206
  29.5 5.3 %copy-start.5 = (s32[8192]{0:T(1024)S(1)}, s32[8192]{0:T(1024)}, u32[]{:S(2)}) copy-start(s32[8192]{0:T(1024)} %param.12) | copy-start | bytes 98308
  34.7 0.7 %copy-start.6 = (s32[1,3]{1,0:T(1,128)S(1)}, s32[1,3]{1,0:T(1,128)}, u32[]{:S(2)}) copy-start(s32[1,3]{1,0:T(1,128)} %visits_ref.1) | copy-start | bytes 40

commit v2 on v1

v2 whole, which is shorter than its diff:
```python
import math

import jax
import jax.numpy as jnp
from jax import lax
from jax.experimental import pallas as pl
from jax.experimental.pallas import tpu as pltpu
from jax.sharding import PartitionSpec as P

HEAD_DIM = 128
BACK = 3
EPSILON = 1e-06
GROUP = 4
F32 = jnp.float32
BF16 = jnp.bfloat16
SCALE = HEAD_DIM**-0.5 * math.log2(math.e)


def dot_nn(left, right):
    return lax.dot_general(left, right, (((1,), (0,)), ((), ())), preferred_element_type=F32)


def dot_nt(left, right):
    return lax.dot_general(left, right, (((1,), (1,)), ((), ())), preferred_element_type=F32)


def columns(head):
    return slice(head * HEAD_DIM, (head + 1) * HEAD_DIM)


def upper_inverse(strict_uppers, row, col):
    size = row.shape[0]
    eye = jnp.where(row == col, 1.0, 0.0).astype(F32)
    base = 16
    same = (row // base) == (col // base)
    diag = [jnp.where(same, u, 0.0) for u in strict_uppers]
    power = [d.astype(BF16) for d in diag]
    inverse = [eye - d for d in diag]
    reach = 2
    while reach < base:
        power = [dot_nn(p, p).astype(BF16) for p in power]
        inverse = [x + dot_nn(x.astype(BF16), p) for x, p in zip(inverse, power)]
        reach *= 2
    span = 2 * base
    while span <= size:
        joined = ((row // span) == (col // span)) & ((row // (span // 2)) != (col // (span // 2)))
        corner = [jnp.where(joined, u, 0.0).astype(BF16) for u in strict_uppers]
        half = [x.astype(BF16) for x in inverse]
        mid = [dot_nn(x, e).astype(BF16) for x, e in zip(half, corner)]
        inverse = [x - dot_nn(m, y) for x, m, y in zip(inverse, mid, half)]
        span *= 2
    return inverse


def prep_kernel(
    k_hbm, w_hbm, beta_hbm, q_hbm, wb_ref, bt_ref, cct_ref, c_ref, d_ref, k_ref, q_ref,
    w_ref, beta_ref, sems,
):
    length, width = k_ref.shape
    copies = [
        pltpu.make_async_copy(w_hbm, w_ref, sems.at[0]),
        pltpu.make_async_copy(beta_hbm, beta_ref, sems.at[2]),
        pltpu.make_async_copy(k_hbm, k_ref, sems.at[1]),
        pltpu.make_async_copy(q_hbm, q_ref, sems.at[3]),
    ]
    for copy in copies:
        copy.start()
    heads = width // HEAD_DIM
    row = lax.broadcasted_iota(jnp.int32, (length, length), 0)
    col = lax.broadcasted_iota(jnp.int32, (length, length), 1)
    upper = row < col
    copies[0].wait()
    copies[1].wait()
    beta = beta_ref[...].astype(F32)
    beta = jnp.transpose(jnp.concatenate([beta] * (length // heads), axis=0))
    units, turned_units, uppers, rights = [], [], [], []
    scaled = []
    for h in range(heads):
        w = w_ref[:, columns(h)].astype(F32)
        scale = lax.rsqrt(jnp.sum(w * w, axis=-1, keepdims=True) + EPSILON)
        unit = w * scale
        wb = unit.astype(BF16)
        bw = unit * beta[:, h : h + 1]
        units.append(wb)
        scaled.append(bw.astype(BF16))
        turned_units.append(jnp.transpose(bw).astype(BF16))
        wb_ref[:, columns(h)] = wb
    copies[2].wait()
    for h in range(heads):
        both = dot_nt(jnp.concatenate([units[h], k_ref[:, columns(h)]], axis=0), scaled[h])
        uppers.append(jnp.where(upper, both[:length], 0.0))
        rights.append(jnp.where(upper, both[length:], 0.0).astype(BF16))
    inverse = upper_inverse(uppers, row, col)
    for h in range(heads):
        solved = dot_nn(
            jnp.concatenate([turned_units[h], rights[h]], axis=0), inverse[h].astype(BF16)
        ).astype(BF16)
        bt_ref[:, columns(h)] = solved[:length]
        cct_ref[:, columns(h)] = solved[length:]
        moved = dot_nn(solved, units[h])
        d_ref[:, columns(h)] = moved[:length].astype(BF16)
        c_ref[:, columns(h)] = (k_ref[:, columns(h)].astype(F32) - moved[length:]).astype(BF16)
    copies[3].wait()


def pair_kernel(c_ref, d_ref, other_ref, _, x2_ref, e_ref):
    length = c_ref.shape[0]
    for h in range(c_ref.shape[1] // HEAD_DIM):
        c, d, o = c_ref[:, columns(h)], d_ref[:, columns(h)], other_ref[:, columns(h)]
        both = dot_nn(jnp.concatenate([c, d], axis=0), o)
        x2_ref[:, columns(h)] = (c.astype(F32) - both[:length]).astype(BF16)
        e_ref[:, columns(h)] = (d.astype(F32) + o.astype(F32) - both[length:]).astype(BF16)


def third_kernel(near_ref, e_ref, x3_ref):
    for h in range(e_ref.shape[1] // HEAD_DIM):
        x = near_ref[:, columns(h)]
        x3_ref[:, columns(h)] = (x.astype(F32) - dot_nn(x, e_ref[:, columns(h)])).astype(BF16)


def query_kernel(
    visits_hbm, seg_ref, q_ref, k_ref, wb_ref, bt_ref, cct_ref, other_ref,
    t_ref, t2_ref, own_ref, gate_ref, visits_ref, sem,
):
    copy = pltpu.make_async_copy(visits_hbm, visits_ref, sem)
    copy.start()
    length, width = q_ref.shape
    row = lax.broadcasted_iota(jnp.int32, (length, length), 0)
    col = lax.broadcasted_iota(jnp.int32, (length, length), 1)
    block = lax.axis_index("seq")
    odd = lax.rem(block, 2)
    for group in range(0, width // HEAD_DIM, GROUP):
        cs = [columns(h) for h in range(group, group + GROUP)]
        both = [
            dot_nt(q_ref[:, c], jnp.concatenate([wb_ref[:, c], k_ref[:, c]], axis=0)) for c in cs
        ]
        query_w = [jnp.where(col <= row, b[:, :length], 0.0) for b in both]
        high = [w.astype(BF16) for w in query_w]
        low = [(w - h.astype(F32)).astype(BF16) for w, h in zip(query_w, high)]
        turn = [
            dot_nt(
                jnp.concatenate([h, w], axis=0),
                jnp.concatenate([bt_ref[:, c], cct_ref[:, c]], axis=0),
            )
            for h, w, c in zip(high, low, cs)
        ]
        turn = [t[:length] + t[length:] for t in turn]
        exact = [(q_ref[:, c].astype(F32) - t[:, :length]) * SCALE for t, c in zip(turn, cs)]
        rounded = [t.astype(BF16) for t in exact]
        shift = [dot_nt(t, other_ref[:, c]) for t, c in zip(rounded, cs)]
        for b, t, e, r, x, c in zip(both, turn, exact, rounded, shift, cs):
            own_ref[:, c] = (b[:, length:] - t[:, length:]) * SCALE
            t_ref[:, c] = r
            t2_ref[:, c] = (e - jnp.where(odd == 1, x, 0.0)).astype(BF16)

    def seg_row(back):
        return seg_ref[pl.ds(jnp.maximum(block - back, 0), 1), :].astype(F32)

    seg_q = jnp.transpose(jnp.broadcast_to(seg_row(0), (length, length)))
    copy.wait()
    for back in range(BACK + 1):
        allowed = seg_q == seg_row(back)
        if back == 0:
            allowed = allowed & (col <= row)
        else:
            allowed = allowed & (jnp.where(block - back >= 0, visits_ref[0, back - 1], 0) > 0)
        gate_ref[back] = jnp.where(allowed, 0.0, -1e30)


def near_kernel(gate_ref, t_ref, own_ref, near_ref, _, __, score_ref):
    for h in range(t_ref.shape[1] // HEAD_DIM):
        c = columns(h)
        score_ref[0, :, c] = own_ref[:, c] + gate_ref[0]
        score_ref[1, :, c] = dot_nt(t_ref[:, c], near_ref[:, c]) + gate_ref[1]


def by_parity(even, odd):
    parity = lax.rem(lax.axis_index("seq"), 2)
    pl.when(parity == 0)(even)
    pl.when(parity == 1)(odd)


def mid_kernel(
    gate_ref, t2_ref, score_ref, v_ref, early_ref, swapped_ref, pair_v_ref, even2, odd2,
    acc_ref, top_ref, total_ref,
):
    def run(far, v1):
        for group in range(0, t2_ref.shape[1] // HEAD_DIM, GROUP):
            cs = [columns(h) for h in range(group, group + GROUP)]
            score = [dot_nt(t2_ref[:, c], far[:, c]) + gate_ref[2] for c in cs]
            score = [
                jnp.concatenate([x, score_ref[1, :, c], score_ref[0, :, c]], axis=1)
                for x, c in zip(score, cs)
            ]
            top = [jnp.max(x, axis=-1, keepdims=True) for x in score]
            weights = [jnp.exp2(x - m) for x, m in zip(score, top)]
            for x, m, c in zip(weights, top, cs):
                rows = [early_ref[:, c], v1[:, c], v_ref[:, c]]
                acc_ref[:, c] = dot_nn(x.astype(BF16), jnp.concatenate(rows, axis=0))
                total = jnp.sum(x, axis=-1, keepdims=True)
                top_ref[:, c] = jnp.broadcast_to(m, acc_ref[:, c].shape)
                total_ref[:, c] = jnp.broadcast_to(total, acc_ref[:, c].shape)

    by_parity(lambda: run(even2, swapped_ref), lambda: run(odd2, pair_v_ref))


def final_kernel(
    gate_ref, t2_ref, acc_ref, top_ref, total_ref, even3, direct, odd3, swapped,
    out_hbm, out_ref, sems,
):
    heads = t2_ref.shape[1] // HEAD_DIM

    def copy(group):
        part = slice(group * HEAD_DIM, (group + GROUP) * HEAD_DIM)
        return pltpu.make_async_copy(out_ref.at[:, part], out_hbm.at[:, part], sems.at[group])

    def run(far, v3):
        for group in range(0, heads, GROUP):
            cs = [columns(h) for h in range(group, group + GROUP)]
            score = [dot_nt(t2_ref[:, c], far[:, c]) + gate_ref[3] for c in cs]
            top = [
                jnp.maximum(jnp.max(x, axis=-1, keepdims=True), top_ref[:, c])
                for x, c in zip(score, cs)
            ]
            weights = [jnp.exp2(x - m) for x, m in zip(score, top)]
            shrink = [jnp.exp2(top_ref[:, c] - m) for m, c in zip(top, cs)]
            mixed = [dot_nn(x.astype(BF16), v3[:, c]) for x, c in zip(weights, cs)]
            for x, m, p, c in zip(weights, mixed, shrink, cs):
                total = jnp.sum(x, axis=-1, keepdims=True) + p * total_ref[:, c]
                out_ref[:, c] = ((m + p * acc_ref[:, c]) / total).astype(BF16)
            copy(group).start()

    by_parity(lambda: run(even3, direct), lambda: run(odd3, swapped))
    for group in range(0, heads, GROUP):
        copy(group).wait()


def call(body, outs, *args, scratch=(), specs=None, out_specs=None, name=None):
    kept = pl.BlockSpec(memory_space=pltpu.VMEM)
    return pl.pallas_call(
        body,
        out_shape=outs,
        in_specs=specs or [kept] * len(args),
        out_specs=out_specs or [kept] * len(outs),
        scratch_shapes=scratch,
        compiler_params=pltpu.CompilerParams(vmem_limit_bytes=32 << 20),
        cost_estimate=pl.CostEstimate(flops=0, bytes_accessed=0, transcendentals=0),
        name=name,
    )(*args)


def shards(queries, keys, values, transitions, betas, segments, visits):
    shape = jax.ShapeDtypeStruct(queries.shape, BF16)
    wide = jax.ShapeDtypeStruct(queries.shape, F32)
    two_wide = jax.ShapeDtypeStruct((2, *queries.shape), F32)
    gates = jax.ShapeDtypeStruct((BACK + 1, queries.shape[0], queries.shape[0]), F32)
    size = lax.axis_size("seq")
    next_one = [(i, i + 1) for i in range(size - 1)]
    odd_three = [(i, i + 3) for i in range(1, size - 3, 2)]
    swap = [(i, i ^ 1) for i in range(size)]
    next_two = [(i, i + 2) for i in range(size - 2)]
    next_even = [(i, i + 2) for i in range(0, size - 2, 2)]
    to_odd = [(i, i + 1) for i in range(0, size, 2)]
    vmem = pl.BlockSpec(memory_space=pltpu.VMEM)
    smem = pl.BlockSpec(memory_space=pltpu.SMEM)
    hbm = pl.BlockSpec(memory_space=pltpu.HBM)
    anywhere = pl.BlockSpec(memory_space=pl.ANY)
    buffer = pltpu.VMEM(queries.shape, BF16)

    def sems(count):
        return pltpu.SemaphoreType.DMA((count,))

    unit, back_t, coef_t, carried, op, keys_, queries_ = call(
        prep_kernel,
        [shape] * 7,
        pltpu.with_memory_space_constraint(keys, pltpu.HBM),
        pltpu.with_memory_space_constraint(transitions, pltpu.HBM),
        pltpu.with_memory_space_constraint(betas.T, pltpu.HBM),
        pltpu.with_memory_space_constraint(queries, pltpu.HBM),
        specs=[hbm] * 4,
        scratch=[buffer, pltpu.VMEM(betas.shape[::-1], BF16), sems(4)],
        name="prep",
    )
    near_k = lax.ppermute(carried, "seq", next_one)
    other = lax.ppermute(op, "seq", swap)
    later, _ = lax.optimization_barrier((values, carried))
    direct = lax.ppermute(later, "seq", odd_three)
    turned, turned2, own, gate = call(
        query_kernel,
        [shape, shape, wide, gates],
        pltpu.with_memory_space_constraint(visits, pltpu.HBM),
        segments.reshape(size, -1),
        queries_,
        keys_,
        unit,
        back_t,
        coef_t,
        other,
        specs=[hbm] + [vmem] * 7,
        scratch=[pltpu.SMEM(visits.shape, jnp.int32), pltpu.SemaphoreType.DMA],
        name="query",
    )
    later, _ = lax.optimization_barrier((values, turned))
    early = lax.ppermute(later, "seq", next_two)
    second, both = call(
        pair_kernel,
        [shape, shape],
        carried,
        op,
        other,
        turned,
        specs=[vmem] * 3 + [anywhere],
        name="pair",
    )
    even2 = lax.ppermute(second, "seq", next_even)
    (third,) = call(
        third_kernel,
        [shape],
        near_k,
        both,
        name="third",
    )
    even3 = lax.ppermute(third, "seq", next_even)
    (scores,) = call(
        near_kernel,
        [two_wide],
        gate,
        turned,
        own,
        near_k,
        third,
        direct,
        specs=[vmem] * 4 + [anywhere] * 2,
        name="near",
    )
    near_k_, early_, values_, _ = lax.optimization_barrier((near_k, early, values, third))
    odd2 = lax.ppermute(near_k_, "seq", to_odd)
    swapped = lax.ppermute(early_, "seq", swap)
    pair_v = lax.ppermute(values_, "seq", swap)
    even2_, scores = lax.optimization_barrier((even2, scores))
    odd3 = lax.ppermute(even2_, "seq", to_odd)
    acc, top, total = call(
        mid_kernel,
        [wide, wide, wide],
        gate,
        turned2,
        scores,
        values,
        early,
        swapped,
        pair_v,
        even2,
        odd2,
        name="mid",
    )
    (out,) = call(
        final_kernel,
        [shape],
        gate,
        turned2,
        acc,
        top,
        total,
        even3,
        direct,
        odd3,
        swapped,
        out_specs=[hbm],
        scratch=[buffer, sems(queries.shape[1] // HEAD_DIM)],
        name="final",
    )
    return out


def solution(mesh):
    return jax.shard_map(
        shards,
        mesh=mesh,
        in_specs=(
            P("seq", "head"),
            P("seq", "head"),
            P("seq", "head"),
            P("seq", "head"),
            P("seq", "head"),
            P(),
            P("seq", None),
        ),
        out_specs=P("seq", "head"),
        check_vma=False,
    )
```

time: 39.6 us -> 33.3 us (0.84)
  the two profiles are of different devices: /device:TPU:136 before, /device:TPU:145 now
where the time goes in v2:
time: 33.3 us; the launch traced here: 33.1 us
  starting transfers between devices  14.4 us (43%)
  waiting for transfers between devices  10.4 us (31%)
  Pallas kernels  8.18 us (25%)
    ppermute x1, waiting for transfers between devices, shards(): early = lax.ppermute(later, 'seq', next_two)  9.14 us
    pallas_call x7, Pallas kernels, call(): pl.pallas_call(body, out_shape=outs, in_specs=specs or [kept] * len(args)...  8.18 us
    ppermute x1, starting transfers between devices, shards(): direct = lax.ppermute(later, 'seq', odd_three)  3.94 us
    ppermute x1, starting transfers between devices, shards(): near_k = lax.ppermute(carried, 'seq', next_one)  3.03 us
    ppermute x1, starting transfers between devices, shards(): early = lax.ppermute(later, 'seq', next_two)  2.21 us
    ppermute x1, starting transfers between devices, shards(): odd3 = lax.ppermute(even2_, 'seq', to_odd)  1.29 us
    ppermute x1, starting transfers between devices, shards(): odd2 = lax.ppermute(near_k_, 'seq', to_odd)  1.28 us
    ppermute x1, waiting for transfers between devices, shards(): odd2 = lax.ppermute(near_k_, 'seq', to_odd)  0.8 us
  transfers between devices with their start and end apart: 10, of which 3 were waited for; matrix products, arithmetic and copies ran while one was open for 0% of the time, Pallas kernels for 8%

profile of v2, /device:TPU:145, one launch (start us, length us, event | category | flops | bytes accessed | tf_op | source)
XLA Modules:
  0.0 33.1 jit_solution(44148798342259757)
XLA Ops:
  0.0 0.0 copy-start
  0.0 0.0 copy-start.1
  0.0 4.0 %prep.1 = (bf16[128,1024]{1,0:T(8,128)(2,1)S(1)}, bf16[128,1024]{1,0:T(8,128)(2,1)S(1)}, bf16[128,1024]{1,0:T(8,128)(2,1)S(1)}, bf16[128,1024]{1,0:T(8,128)(2,1)...) custom-call(bf16[128,1024]{1,0:T(8,128)(2,1)} %k_hbm.1, ...), custom_call_target="tpu_custom_call" | custom-call | tf_op jit(solution)/shard_map/prep/pallas_call | solution.py:240
  4.0 0.8 %collective-permute-start = (bf16[128,1024]{1,0:T(8,128)(2,1)S(1)}, bf16[128,1024]{1,0:T(8,128)(2,1)S(1)}, u32[]{:S(2)}, u32[]{:S(2)}) collective-permute-start(bf16[128,1024]{1,0:T(8,128)(2,1)S(1)} %get-tuple-element.33.d_ref), channel_id=1, source_target_pairs={{0,4},{4,0},{8,12},{12,8},{16,20},{20,16},{24,28},{28,24},{32,36},... | collective-permute-start | bytes 786440 | tf_op jit(solution)/shard_map/ppermute | solution.py:285
  4.7 3.0 %collective-permute-start.2 = (bf16[128,1024]{1,0:T(8,128)(2,1)S(1)}, bf16[128,1024]{1,0:T(8,128)(2,1)S(1)}, u32[]{:S(2)}, u32[]{:S(2)}) collective-permute-start(bf16[128,1024]{1,0:T(8,128)(2,1)S(1)} %get-tuple-element.36.c_ref), channel_id=1, source_target_pairs={{0,4},{4,8},{8,12},{12,16},{16,20},{20,24},{24,28},{28,32},{32,36}... | collective-permute-start | bytes 786440 | tf_op jit(solution)/shard_map/ppermute | solution.py:284
  7.8 0.0 copy-done
  7.8 3.9 %collective-permute-start.3 = (bf16[128,1024]{1,0:T(8,128)(2,1)S(1)}, bf16[128,1024]{1,0:T(8,128)(2,1)S(1)}, u32[]{:S(2)}, u32[]{:S(2)}) collective-permute-start(bf16[128,1024]{1,0:T(8,128)(2,1)S(1)} %copy-done), channel_id=1, source_target_pairs={{4,16},{12,24},{20,32},{28,40},{36,48},{44,56},{52,64},{60,72},{68... | collective-permute-start | bytes 786440 | tf_op jit(solution)/shard_map/ppermute | solution.py:287
  11.7 0.0 collective-permute-done.other_ref
  11.7 0.0 copy-done.1
  11.8 1.0 %query.1 = (bf16[128,1024]{1,0:T(8,128)(2,1)S(1)}, bf16[128,1024]{1,0:T(8,128)(2,1)S(1)}, f32[128,1024]{1,0:T(8,128)S(1)}, f32[4,128,128]{2,1,0:T(8,128)S(1)}) custom-call(s32[1,3]{1,0:T(1,128)} %visits_hbm.1, s32[64,128]{1,0:T(8,128)S(1)} %bitcast.2, bf16[128,1024]{1,0:T(8,128)(2,1)S(1)} %get-tuple-element.28.q_ref, ...), custom_call_target="tpu_custom_call" | custom-call | tf_op jit(solution)/shard_map/query/pallas_call | solution.py:240
  12.8 2.2 %collective-permute-start.4 = (bf16[128,1024]{1,0:T(8,128)(2,1)S(1)}, bf16[128,1024]{1,0:T(8,128)(2,1)S(1)}, u32[]{:S(2)}, u32[]{:S(2)}) collective-permute-start(bf16[128,1024]{1,0:T(8,128)(2,1)S(1)} %copy-done), channel_id=1, source_target_pairs={{0,8},{4,12},{8,16},{12,20},{16,24},{20,28},{24,32},{28,36},{32,40... | collective-permute-start | bytes 786440 | tf_op jit(solution)/shard_map/ppermute | solution.py:304
  15.0 0.3 pair.1
  15.3 0.7 %collective-permute-start.1 = (bf16[128,1024]{1,0:T(8,128)(2,1)S(1)}, bf16[128,1024]{1,0:T(8,128)(2,1)S(1)}, u32[]{:S(2)}, u32[]{:S(2)}) collective-permute-start(bf16[128,1024]{1,0:T(8,128)(2,1)S(1)} %get-tuple-element.38), channel_id=1, source_target_pairs={{0,8},{8,16},{16,24},{24,32},{32,40},{40,48},{48,56},{56,64},{64,7... | collective-permute-start | bytes 786440 | tf_op jit(solution)/shard_map/ppermute | solution.py:315
  16.0 0.0 collective-permute-done.2.near_ref
  16.0 0.2 third.1._
  16.2 0.7 %collective-permute-start.8 = (bf16[128,1024]{1,0:T(8,128)(2,1)S(1)}, bf16[128,1024]{1,0:T(8,128)(2,1)S(1)}, u32[]{:S(2)}, u32[]{:S(2)}) collective-permute-start(bf16[128,1024]{1,0:T(8,128)(2,1)S(1)} %third.1._), channel_id=1, source_target_pairs={{0,8},{8,16},{16,24},{24,32},{32,40},{40,48},{48,56},{56,64},{64,7... | collective-permute-start | bytes 786440 | tf_op jit(solution)/shard_map/ppermute | solution.py:323
  16.9 0.0 collective-permute-done.3.__.direct
  16.9 0.3 near.1.score_ref
  17.3 9.1 %collective-permute-done.4.early_ref = bf16[128,1024]{1,0:T(8,128)(2,1)S(1)} collective-permute-done((bf16[128,1024]{1,0:T(8,128)(2,1)S(1)}, bf16[128,1024]{1,0:T(8,128)(2,1)S(1)}, u32[]{:S(2)}, u32[]{:S(2)}) %collective-permute-start.4) | collective-permute-done | bytes 262176 | tf_op jit(solution)/shard_map/ppermute | solution.py:304
  26.4 0.0 collective-permute-start.5
  26.4 0.5 %collective-permute-start.6 = (bf16[128,1024]{1,0:T(8,128)(2,1)S(1)}, bf16[128,1024]{1,0:T(8,128)(2,1)S(1)}, u32[]{:S(2)}, u32[]{:S(2)}) collective-permute-start(bf16[128,1024]{1,0:T(8,128)(2,1)S(1)} %copy-done), channel_id=1, source_target_pairs={{0,4},{4,0},{8,12},{12,8},{16,20},{20,16},{24,28},{28,24},{32,36},... | collective-permute-start | bytes 786440 | tf_op jit(solution)/shard_map/ppermute | solution.py:339
  26.9 1.3 %collective-permute-start.7 = (bf16[128,1024]{1,0:T(8,128)(2,1)S(1)}, bf16[128,1024]{1,0:T(8,128)(2,1)S(1)}, u32[]{:S(2)}, u32[]{:S(2)}) collective-permute-start(bf16[128,1024]{1,0:T(8,128)(2,1)S(1)} %collective-permute-done.2.near_ref), channel_id=1, source_target_pairs={{0,4},{8,12},{16,20},{24,28},{32,36},{40,44},{48,52},{56,60},{64,6... | collective-permute-start | bytes 786440 | tf_op jit(solution)/shard_map/ppermute | solution.py:337
  28.2 0.0 collective-permute-done.1.even2
  28.2 1.3 %collective-permute-start.9 = (bf16[128,1024]{1,0:T(8,128)(2,1)S(1)}, bf16[128,1024]{1,0:T(8,128)(2,1)S(1)}, u32[]{:S(2)}, u32[]{:S(2)}) collective-permute-start(bf16[128,1024]{1,0:T(8,128)(2,1)S(1)} %collective-permute-done.1.even2), channel_id=1, source_target_pairs={{0,4},{8,12},{16,20},{24,28},{32,36},{40,44},{48,52},{56,60},{64,6... | collective-permute-start | bytes 786440 | tf_op jit(solution)/shard_map/ppermute | solution.py:341
  29.5 0.0 collective-permute-done.5.swapped_ref.swapped
  29.5 0.0 collective-permute-done.6.pair_v_ref
  29.5 0.8 %collective-permute-done.7.odd2 = bf16[128,1024]{1,0:T(8,128)(2,1)S(1)} collective-permute-done((bf16[128,1024]{1,0:T(8,128)(2,1)S(1)}, bf16[128,1024]{1,0:T(8,128)(2,1)S(1)}, u32[]{:S(2)}, u32[]{:S(2)}) %collective-permute-start.7) | collective-permute-done | bytes 262176 | tf_op jit(solution)/shard_map/ppermute | solution.py:337
  30.3 0.9 %mid.1 = (f32[128,1024]{1,0:T(8,128)S(1)}, f32[128,1024]{1,0:T(8,128)S(1)}, f32[128,1024]{1,0:T(8,128)S(1)}) custom-call(f32[4,128,128]{2,1,0:T(8,128)S(1)} %get-tuple-element.34.gate_ref, bf16[128,1024]{1,0:T(8,128)(2,1)S(1)} %get-tuple-element.35.t2_ref, f32[2,128,1024]{2,1,0:T(8,128)S(1)} %near.1.score_ref, bf16[128,1024]{1,0:T(8,128)(2,1)S(1)} %copy-done, ...), custom_call_target="tpu_custom_call" | custom-call | tf_op jit(solution)/shard_map/mid/pallas_call | solution.py:240
  31.2 0.0 collective-permute-done.8.even3
  31.2 0.4 %collective-permute-done.9.odd3 = bf16[128,1024]{1,0:T(8,128)(2,1)S(1)} collective-permute-done((bf16[128,1024]{1,0:T(8,128)(2,1)S(1)}, bf16[128,1024]{1,0:T(8,128)(2,1)S(1)}, u32[]{:S(2)}, u32[]{:S(2)}) %collective-permute-start.9) | collective-permute-done | bytes 262176 | tf_op jit(solution)/shard_map/ppermute | solution.py:341
  31.7 1.4 %final.1 = bf16[128,1024]{1,0:T(8,128)(2,1)} custom-call(f32[4,128,128]{2,1,0:T(8,128)S(1)} %get-tuple-element.34.gate_ref, bf16[128,1024]{1,0:T(8,128)(2,1)S(1)} %get-tuple-element.35.t2_ref, f32[128,1024]{1,0:T(8,128)S(1)} %get-tuple-element.47.acc_ref, f32[128,1024]{1,0:T(8,128)S(1)} %get-tuple-element.48.top_ref, ...), custom_call_target="tpu_custom_call" | custom-call | tf_op jit(solution)/shard_map/final/pallas_call | solution.py:240
Async XLA Ops:
  0.0 7.8 %copy-start = (bf16[128,1024]{1,0:T(8,128)(2,1)S(1)}, bf16[128,1024]{1,0:T(8,128)(2,1)}, u32[]{:S(2)}) copy-start(bf16[128,1024]{1,0:T(8,128)(2,1)} %v_ref.1) | copy-start | bytes 786436
  0.0 11.7 %copy-start.1 = (s32[8192]{0:T(1024)S(1)}, s32[8192]{0:T(1024)}, u32[]{:S(2)}) copy-start(s32[8192]{0:T(1024)} %param.12) | copy-start | bytes 98308
  4.0 7.7 %collective-permute-start = (bf16[128,1024]{1,0:T(8,128)(2,1)S(1)}, bf16[128,1024]{1,0:T(8,128)(2,1)S(1)}, u32[]{:S(2)}, u32[]{:S(2)}) collective-permute-start(bf16[128,1024]{1,0:T(8,128)(2,1)S(1)} %get-tuple-element.33.d_ref), channel_id=1, source_target_pairs={{0,4},{4,0},{8,12},{12,8},{16,20},{20,16},{24,28},{28,24},{32,36},... | collective-permute-start | bytes 786440 | tf_op jit(solution)/shard_map/ppermute | solution.py:285
  4.7 11.3 %collective-permute-start.2 = (bf16[128,1024]{1,0:T(8,128)(2,1)S(1)}, bf16[128,1024]{1,0:T(8,128)(2,1)S(1)}, u32[]{:S(2)}, u32[]{:S(2)}) collective-permute-start(bf16[128,1024]{1,0:T(8,128)(2,1)S(1)} %get-tuple-element.36.c_ref), channel_id=1, source_target_pairs={{0,4},{4,8},{8,12},{12,16},{16,20},{20,24},{24,28},{28,32},{32,36}... | collective-permute-start | bytes 786440 | tf_op jit(solution)/shard_map/ppermute | solution.py:284
  7.8 9.1 %collective-permute-start.3 = (bf16[128,1024]{1,0:T(8,128)(2,1)S(1)}, bf16[128,1024]{1,0:T(8,128)(2,1)S(1)}, u32[]{:S(2)}, u32[]{:S(2)}) collective-permute-start(bf16[128,1024]{1,0:T(8,128)(2,1)S(1)} %copy-done), channel_id=1, source_target_pairs={{4,16},{12,24},{20,32},{28,40},{36,48},{44,56},{52,64},{60,72},{68... | collective-permute-start | bytes 786440 | tf_op jit(solution)/shard_map/ppermute | solution.py:287
  12.8 13.6 %collective-permute-start.4 = (bf16[128,1024]{1,0:T(8,128)(2,1)S(1)}, bf16[128,1024]{1,0:T(8,128)(2,1)S(1)}, u32[]{:S(2)}, u32[]{:S(2)}) collective-permute-start(bf16[128,1024]{1,0:T(8,128)(2,1)S(1)} %copy-done), channel_id=1, source_target_pairs={{0,8},{4,12},{8,16},{12,20},{16,24},{20,28},{24,32},{28,36},{32,40... | collective-permute-start | bytes 786440 | tf_op jit(solution)/shard_map/ppermute | solution.py:304
  15.3 12.9 %collective-permute-start.1 = (bf16[128,1024]{1,0:T(8,128)(2,1)S(1)}, bf16[128,1024]{1,0:T(8,128)(2,1)S(1)}, u32[]{:S(2)}, u32[]{:S(2)}) collective-permute-start(bf16[128,1024]{1,0:T(8,128)(2,1)S(1)} %get-tuple-element.38), channel_id=1, source_target_pairs={{0,8},{8,16},{16,24},{24,32},{32,40},{40,48},{48,56},{56,64},{64,7... | collective-permute-start | bytes 786440 | tf_op jit(solution)/shard_map/ppermute | solution.py:315
  16.2 15.0 %collective-permute-start.8 = (bf16[128,1024]{1,0:T(8,128)(2,1)S(1)}, bf16[128,1024]{1,0:T(8,128)(2,1)S(1)}, u32[]{:S(2)}, u32[]{:S(2)}) collective-permute-start(bf16[128,1024]{1,0:T(8,128)(2,1)S(1)} %third.1._), channel_id=1, source_target_pairs={{0,8},{8,16},{16,24},{24,32},{32,40},{40,48},{48,56},{56,64},{64,7... | collective-permute-start | bytes 786440 | tf_op jit(solution)/shard_map/ppermute | solution.py:323
  26.4 3.1 %collective-permute-start.5 = (bf16[128,1024]{1,0:T(8,128)(2,1)S(1)}, bf16[128,1024]{1,0:T(8,128)(2,1)S(1)}, u32[]{:S(2)}, u32[]{:S(2)}) collective-permute-start(bf16[128,1024]{1,0:T(8,128)(2,1)S(1)} %collective-permute-done.4.early_ref), channel_id=1, source_target_pairs={{0,4},{4,0},{8,12},{12,8},{16,20},{20,16},{24,28},{28,24},{32,36},... | collective-permute-start | bytes 786440 | tf_op jit(solution)/shard_map/ppermute | solution.py:338
  26.4 3.1 %collective-permute-start.6 = (bf16[128,1024]{1,0:T(8,128)(2,1)S(1)}, bf16[128,1024]{1,0:T(8,128)(2,1)S(1)}, u32[]{:S(2)}, u32[]{:S(2)}) collective-permute-start(bf16[128,1024]{1,0:T(8,128)(2,1)S(1)} %copy-done), channel_id=1, source_target_pairs={{0,4},{4,0},{8,12},{12,8},{16,20},{20,16},{24,28},{28,24},{32,36},... | collective-permute-start | bytes 786440 | tf_op jit(solution)/shard_map/ppermute | solution.py:339
  26.9 3.4 %collective-permute-start.7 = (bf16[128,1024]{1,0:T(8,128)(2,1)S(1)}, bf16[128,1024]{1,0:T(8,128)(2,1)S(1)}, u32[]{:S(2)}, u32[]{:S(2)}) collective-permute-start(bf16[128,1024]{1,0:T(8,128)(2,1)S(1)} %collective-permute-done.2.near_ref), channel_id=1, source_target_pairs={{0,4},{8,12},{16,20},{24,28},{32,36},{40,44},{48,52},{56,60},{64,6... | collective-permute-start | bytes 786440 | tf_op jit(solution)/shard_map/ppermute | solution.py:337
  28.2 3.4 %collective-permute-start.9 = (bf16[128,1024]{1,0:T(8,128)(2,1)S(1)}, bf16[128,1024]{1,0:T(8,128)(2,1)S(1)}, u32[]{:S(2)}, u32[]{:S(2)}) collective-permute-start(bf16[128,1024]{1,0:T(8,128)(2,1)S(1)} %collective-permute-done.1.even2), channel_id=1, source_target_pairs={{0,4},{8,12},{16,20},{24,28},{32,36},{40,44},{48,52},{56,60},{64,6... | collective-permute-start | bytes 786440 | tf_op jit(solution)/shard_map/ppermute | solution.py:341

commit v3 on v2

--- a/solution.py
+++ b/solution.py
@@ -28,26 +28,47 @@
     return slice(head * HEAD_DIM, (head + 1) * HEAD_DIM)
 
 
+def pairs(width):
+    return [slice(at, at + 2 * HEAD_DIM) for at in range(0, width, 2 * HEAD_DIM)]
+
+
+def blocks(two):
+    zero = jnp.zeros((two.shape[0], HEAD_DIM), two.dtype)
+    return jnp.concatenate(
+        [
+            jnp.concatenate([two[:, :HEAD_DIM], zero], axis=1),
+            jnp.concatenate([zero, two[:, HEAD_DIM:]], axis=1),
+        ],
+        axis=0,
+    )
+
+
 def upper_inverse(strict_uppers, row, col):
     size = row.shape[0]
     eye = jnp.where(row == col, 1.0, 0.0).astype(F32)
     base = 16
     same = (row // base) == (col // base)
     diag = [jnp.where(same, u, 0.0) for u in strict_uppers]
-    power = [d.astype(BF16) for d in diag]
+    first = [d.astype(BF16) for d in diag]
+    power = [dot_nn(p, blocks(p)).astype(BF16) for p in first]
     inverse = [eye - d for d in diag]
-    reach = 2
+    reach = 4
     while reach < base:
-        power = [dot_nn(p, p).astype(BF16) for p in power]
-        inverse = [x + dot_nn(x.astype(BF16), p) for x, p in zip(inverse, power)]
+        both = [
+            dot_nn(jnp.concatenate([x.astype(BF16), p], axis=0), blocks(p))
+            for x, p in zip(inverse, power)
+        ]
+        inverse = [x + b[:size] for x, b in zip(inverse, both)]
+        power = [b[size:].astype(BF16) for b in both]
         reach *= 2
+    inverse = [x + dot_nn(x.astype(BF16), blocks(p)) for x, p in zip(inverse, power)]
     span = 2 * base
     while span <= size:
         joined = ((row // span) == (col // span)) & ((row // (span // 2)) != (col // (span // 2)))
         corner = [jnp.where(joined, u, 0.0).astype(BF16) for u in strict_uppers]
         half = [x.astype(BF16) for x in inverse]
-        mid = [dot_nn(x, e).astype(BF16) for x, e in zip(half, corner)]
-        inverse = [x - dot_nn(m, y) for x, m, y in zip(inverse, mid, half)]
+        mid = [dot_nn(x, blocks(e)).astype(BF16) for x, e in zip(half, corner)]
+        inverse = [x - dot_nn(m, blocks(y)) for x, m, y in zip(inverse, mid, half)]
         span *= 2
     return inverse
 
@@ -66,40 +87,41 @@
     for copy in copies:
         copy.start()
     heads = width // HEAD_DIM
-    row = lax.broadcasted_iota(jnp.int32, (length, length), 0)
-    col = lax.broadcasted_iota(jnp.int32, (length, length), 1)
+    row = lax.broadcasted_iota(jnp.int32, (length, 2 * length), 0)
+    col = lax.rem(lax.broadcasted_iota(jnp.int32, (length, 2 * length), 1), length)
     upper = row < col
     copies[0].wait()
     copies[1].wait()
     beta = beta_ref[...].astype(F32)
     beta = jnp.transpose(jnp.concatenate([beta] * (length // heads), axis=0))
-    units, turned_units, uppers, rights = [], [], [], []
-    scaled = []
+    scaled, turned_units = [], []
     for h in range(heads):
         w = w_ref[:, columns(h)].astype(F32)
         scale = lax.rsqrt(jnp.sum(w * w, axis=-1, keepdims=True) + EPSILON)
         unit = w * scale
-        wb = unit.astype(BF16)
         bw = unit * beta[:, h : h + 1]
-        units.append(wb)
         scaled.append(bw.astype(BF16))
         turned_units.append(jnp.transpose(bw).astype(BF16))
-        wb_ref[:, columns(h)] = wb
+        wb_ref[:, columns(h)] = unit.astype(BF16)
     copies[2].wait()
-    for h in range(heads):
-        both = dot_nt(jnp.concatenate([units[h], k_ref[:, columns(h)]], axis=0), scaled[h])
-        uppers.append(jnp.where(upper, both[:length], 0.0))
-        rights.append(jnp.where(upper, both[length:], 0.0).astype(BF16))
+    both = []
+    for i, c in enumerate(pairs(width)):
+        right = blocks(jnp.concatenate(scaled[2 * i : 2 * i + 2], axis=1))
+        both.append(dot_nt(jnp.concatenate([wb_ref[:, c], k_ref[:, c]], axis=0), right))
+    uppers = [jnp.where(upper, b[:length], 0.0) for b in both]
+    rights = [jnp.where(upper, b[length:], 0.0).astype(BF16) for b in both]
     inverse = upper_inverse(uppers, row, col)
-    for h in range(heads):
-        solved = dot_nn(
-            jnp.concatenate([turned_units[h], rights[h]], axis=0), inverse[h].astype(BF16)
-        ).astype(BF16)
-        bt_ref[:, columns(h)] = solved[:length]
-        cct_ref[:, columns(h)] = solved[length:]
-        moved = dot_nn(solved, units[h])
-        d_ref[:, columns(h)] = moved[:length].astype(BF16)
-        c_ref[:, columns(h)] = (k_ref[:, columns(h)].astype(F32) - moved[length:]).astype(BF16)
+    solved = []
+    for i, (r, x) in enumerate(zip(rights, inverse)):
+        left = jnp.concatenate(turned_units[2 * i : 2 * i + 2], axis=1)
+        left = jnp.concatenate([left, r], axis=0)
+        solved.append(dot_nn(left, blocks(x.astype(BF16))).astype(BF16))
+    for c, x in zip(pairs(width), solved):
+        moved = dot_nn(x, blocks(wb_ref[:, c]))
+        c_ref[:, c] = (k_ref[:, c].astype(F32) - moved[length:]).astype(BF16)
+        d_ref[:, c] = moved[:length].astype(BF16)
+        bt_ref[:, c] = x[:length]
+        cct_ref[:, c] = x[length:]
     copies[3].wait()
 
 
@@ -113,9 +135,9 @@
 
 
 def third_kernel(near_ref, e_ref, x3_ref):
-    for h in range(e_ref.shape[1] // HEAD_DIM):
-        x = near_ref[:, columns(h)]
-        x3_ref[:, columns(h)] = (x.astype(F32) - dot_nn(x, e_ref[:, columns(h)])).astype(BF16)
+    for c in pairs(e_ref.shape[1]):
+        x = near_ref[:, c]
+        x3_ref[:, c] = (x.astype(F32) - dot_nn(x, blocks(e_ref[:, c]))).astype(BF16)
 
 
 def query_kernel(
@@ -284,7 +306,7 @@
     near_k = lax.ppermute(carried, "seq", next_one)
     other = lax.ppermute(op, "seq", swap)
     later, _ = lax.optimization_barrier((values, carried))
-    direct = lax.ppermute(later, "seq", odd_three)
+    early = lax.ppermute(later, "seq", next_two)
     turned, turned2, own, gate = call(
         query_kernel,
         [shape, shape, wide, gates],
@@ -301,7 +323,7 @@
         name="query",
     )
     later, _ = lax.optimization_barrier((values, turned))
-    early = lax.ppermute(later, "seq", next_two)
+    direct = lax.ppermute(later, "seq", odd_three)
     second, both = call(
         pair_kernel,
         [shape, shape],

time: 33.3 us -> 31.6 us (0.949)
  the two profiles are of different devices: /device:TPU:145 before, /device:TPU:139 now
where the time goes in v3:
time: 31.6 us; the launch traced here: 31.4 us
  starting transfers between devices  15.6 us (49%)
  Pallas kernels  8.13 us (26%)
  waiting for transfers between devices  7.52 us (24%)
    pallas_call x7, Pallas kernels, call(): pl.pallas_call(body, out_shape=outs, in_specs=specs or [kept] * len(args)...  8.13 us
    ppermute x1, waiting for transfers between devices, shards(): odd2 = lax.ppermute(near_k_, 'seq', to_odd)  5.73 us
    ppermute x1, starting transfers between devices, shards(): direct = lax.ppermute(later, 'seq', odd_three)  3.08 us
    ppermute x1, starting transfers between devices, shards(): near_k = lax.ppermute(carried, 'seq', next_one)  3.02 us
    ppermute x1, starting transfers between devices, shards(): early = lax.ppermute(later, 'seq', next_two)  2.83 us
    ppermute x1, starting transfers between devices, shards(): swapped = lax.ppermute(early_, 'seq', swap)  1.87 us
    ppermute x1, starting transfers between devices, shards(): odd3 = lax.ppermute(even2_, 'seq', to_odd)  1.29 us
    ppermute x1, starting transfers between devices, shards(): odd2 = lax.ppermute(near_k_, 'seq', to_odd)  1.28 us
  transfers between devices with their start and end apart: 10, of which 3 were waited for; matrix products, arithmetic and copies ran while one was open for 0% of the time, Pallas kernels for 9%

profile of v3, /device:TPU:139, one launch (start us, length us, event | category | flops | bytes accessed | tf_op | source)
XLA Modules:
  0.0 31.4 jit_solution(6216435337418228451)
XLA Ops:
  0.0 0.0 copy-start
  0.0 0.0 copy-start.1
  0.0 3.9 %prep.1 = (bf16[128,1024]{1,0:T(8,128)(2,1)S(1)}, bf16[128,1024]{1,0:T(8,128)(2,1)S(1)}, bf16[128,1024]{1,0:T(8,128)(2,1)S(1)}, bf16[128,1024]{1,0:T(8,128)(2,1)...) custom-call(bf16[128,1024]{1,0:T(8,128)(2,1)} %k_hbm.1, ...), custom_call_target="tpu_custom_call" | custom-call | tf_op jit(solution)/shard_map/prep/pallas_call | solution.py:262
  3.9 0.8 %collective-permute-start = (bf16[128,1024]{1,0:T(8,128)(2,1)S(1)}, bf16[128,1024]{1,0:T(8,128)(2,1)S(1)}, u32[]{:S(2)}, u32[]{:S(2)}) collective-permute-start(bf16[128,1024]{1,0:T(8,128)(2,1)S(1)} %get-tuple-element.33.d_ref), channel_id=1, source_target_pairs={{0,4},{4,0},{8,12},{12,8},{16,20},{20,16},{24,28},{28,24},{32,36},... | collective-permute-start | bytes 786440 | tf_op jit(solution)/shard_map/ppermute | solution.py:307
  4.7 3.0 %collective-permute-start.2 = (bf16[128,1024]{1,0:T(8,128)(2,1)S(1)}, bf16[128,1024]{1,0:T(8,128)(2,1)S(1)}, u32[]{:S(2)}, u32[]{:S(2)}) collective-permute-start(bf16[128,1024]{1,0:T(8,128)(2,1)S(1)} %get-tuple-element.36.c_ref), channel_id=1, source_target_pairs={{0,4},{4,8},{8,12},{12,16},{16,20},{20,24},{24,28},{28,32},{32,36}... | collective-permute-start | bytes 786440 | tf_op jit(solution)/shard_map/ppermute | solution.py:306
  7.7 0.0 copy-done
  7.7 2.8 %collective-permute-start.4 = (bf16[128,1024]{1,0:T(8,128)(2,1)S(1)}, bf16[128,1024]{1,0:T(8,128)(2,1)S(1)}, u32[]{:S(2)}, u32[]{:S(2)}) collective-permute-start(bf16[128,1024]{1,0:T(8,128)(2,1)S(1)} %copy-done), channel_id=1, source_target_pairs={{0,8},{4,12},{8,16},{12,20},{16,24},{20,28},{24,32},{28,36},{32,40... | collective-permute-start | bytes 786440 | tf_op jit(solution)/shard_map/ppermute | solution.py:309
  10.6 0.0 collective-permute-done.other_ref
  10.6 0.0 copy-done.1
  10.6 1.0 %query.1 = (bf16[128,1024]{1,0:T(8,128)(2,1)S(1)}, bf16[128,1024]{1,0:T(8,128)(2,1)S(1)}, f32[128,1024]{1,0:T(8,128)S(1)}, f32[4,128,128]{2,1,0:T(8,128)S(1)}) custom-call(s32[1,3]{1,0:T(1,128)} %visits_hbm.1, s32[64,128]{1,0:T(8,128)S(1)} %bitcast.2, bf16[128,1024]{1,0:T(8,128)(2,1)S(1)} %get-tuple-element.28.q_ref, ...), custom_call_target="tpu_custom_call" | custom-call | tf_op jit(solution)/shard_map/query/pallas_call | solution.py:262
  11.6 3.1 %collective-permute-start.3 = (bf16[128,1024]{1,0:T(8,128)(2,1)S(1)}, bf16[128,1024]{1,0:T(8,128)(2,1)S(1)}, u32[]{:S(2)}, u32[]{:S(2)}) collective-permute-start(bf16[128,1024]{1,0:T(8,128)(2,1)S(1)} %copy-done), channel_id=1, source_target_pairs={{4,16},{12,24},{20,32},{28,40},{36,48},{44,56},{52,64},{60,72},{68... | collective-permute-start | bytes 786440 | tf_op jit(solution)/shard_map/ppermute | solution.py:326
  14.7 0.3 pair.1
  15.0 0.7 %collective-permute-start.1 = (bf16[128,1024]{1,0:T(8,128)(2,1)S(1)}, bf16[128,1024]{1,0:T(8,128)(2,1)S(1)}, u32[]{:S(2)}, u32[]{:S(2)}) collective-permute-start(bf16[128,1024]{1,0:T(8,128)(2,1)S(1)} %get-tuple-element.38), channel_id=1, source_target_pairs={{0,8},{8,16},{16,24},{24,32},{32,40},{40,48},{48,56},{56,64},{64,7... | collective-permute-start | bytes 786440 | tf_op jit(solution)/shard_map/ppermute | solution.py:337
  15.7 0.0 collective-permute-done.2.near_ref
  15.7 0.2 third.1._
  15.9 0.7 %collective-permute-start.8 = (bf16[128,1024]{1,0:T(8,128)(2,1)S(1)}, bf16[128,1024]{1,0:T(8,128)(2,1)S(1)}, u32[]{:S(2)}, u32[]{:S(2)}) collective-permute-start(bf16[128,1024]{1,0:T(8,128)(2,1)S(1)} %third.1._), channel_id=1, source_target_pairs={{0,8},{8,16},{16,24},{24,32},{32,40},{40,48},{48,56},{56,64},{64,7... | collective-permute-start | bytes 786440 | tf_op jit(solution)/shard_map/ppermute | solution.py:345
  16.6 1.0 %collective-permute-done.4.early_ref = bf16[128,1024]{1,0:T(8,128)(2,1)S(1)} collective-permute-done((bf16[128,1024]{1,0:T(8,128)(2,1)S(1)}, bf16[128,1024]{1,0:T(8,128)(2,1)S(1)}, u32[]{:S(2)}, u32[]{:S(2)}) %collective-permute-start.4) | collective-permute-done | bytes 262176 | tf_op jit(solution)/shard_map/ppermute | solution.py:309
  17.7 1.9 %collective-permute-start.5 = (bf16[128,1024]{1,0:T(8,128)(2,1)S(1)}, bf16[128,1024]{1,0:T(8,128)(2,1)S(1)}, u32[]{:S(2)}, u32[]{:S(2)}) collective-permute-start(bf16[128,1024]{1,0:T(8,128)(2,1)S(1)} %collective-permute-done.4.early_ref), channel_id=1, source_target_pairs={{0,4},{4,0},{8,12},{12,8},{16,20},{20,16},{24,28},{28,24},{32,36},... | collective-permute-start | bytes 786440 | tf_op jit(solution)/shard_map/ppermute | solution.py:360
  19.5 0.1 collective-permute-start.6
  19.6 0.0 collective-permute-done.3.__.direct
  19.6 1.3 %collective-permute-start.7 = (bf16[128,1024]{1,0:T(8,128)(2,1)S(1)}, bf16[128,1024]{1,0:T(8,128)(2,1)S(1)}, u32[]{:S(2)}, u32[]{:S(2)}) collective-permute-start(bf16[128,1024]{1,0:T(8,128)(2,1)S(1)} %collective-permute-done.2.near_ref), channel_id=1, source_target_pairs={{0,4},{8,12},{16,20},{24,28},{32,36},{40,44},{48,52},{56,60},{64,6... | collective-permute-start | bytes 786440 | tf_op jit(solution)/shard_map/ppermute | solution.py:359
  20.9 0.3 %near.1.score_ref = f32[2,128,1024]{2,1,0:T(8,128)S(1)} custom-call(f32[4,128,128]{2,1,0:T(8,128)S(1)} %get-tuple-element.34.gate_ref, bf16[128,1024]{1,0:T(8,128)(2,1)S(1)} %get-tuple-element.37._.t_ref, f32[128,1024]{1,0:T(8,128)S(1)} %get-tuple-element.39.own_ref, bf16[128,1024]{1,0:T(8,128)(2,1)S(1)} %collective-permute-done.2.near_ref, ...), custom_call_target="tpu_custom_call" | custom-call | tf_op jit(solution)/shard_map/near/pallas_call | solution.py:262
  21.2 0.0 collective-permute-done.1.even2
  21.3 1.3 %collective-permute-start.9 = (bf16[128,1024]{1,0:T(8,128)(2,1)S(1)}, bf16[128,1024]{1,0:T(8,128)(2,1)S(1)}, u32[]{:S(2)}, u32[]{:S(2)}) collective-permute-start(bf16[128,1024]{1,0:T(8,128)(2,1)S(1)} %collective-permute-done.1.even2), channel_id=1, source_target_pairs={{0,4},{8,12},{16,20},{24,28},{32,36},{40,44},{48,52},{56,60},{64,6... | collective-permute-start | bytes 786440 | tf_op jit(solution)/shard_map/ppermute | solution.py:363
  22.6 0.0 collective-permute-done.5.swapped_ref.swapped
  22.6 0.0 collective-permute-done.6.pair_v_ref
  22.6 5.7 %collective-permute-done.7.odd2 = bf16[128,1024]{1,0:T(8,128)(2,1)S(1)} collective-permute-done((bf16[128,1024]{1,0:T(8,128)(2,1)S(1)}, bf16[128,1024]{1,0:T(8,128)(2,1)S(1)}, u32[]{:S(2)}, u32[]{:S(2)}) %collective-permute-start.7) | collective-permute-done | bytes 262176 | tf_op jit(solution)/shard_map/ppermute | solution.py:359
  28.3 0.9 %mid.1 = (f32[128,1024]{1,0:T(8,128)S(1)}, f32[128,1024]{1,0:T(8,128)S(1)}, f32[128,1024]{1,0:T(8,128)S(1)}) custom-call(f32[4,128,128]{2,1,0:T(8,128)S(1)} %get-tuple-element.34.gate_ref, bf16[128,1024]{1,0:T(8,128)(2,1)S(1)} %get-tuple-element.35.t2_ref, f32[2,128,1024]{2,1,0:T(8,128)S(1)} %near.1.score_ref, bf16[128,1024]{1,0:T(8,128)(2,1)S(1)} %copy-done, ...), custom_call_target="tpu_custom_call" | custom-call | tf_op jit(solution)/shard_map/mid/pallas_call | solution.py:262
  29.2 0.0 collective-permute-done.8.even3
  29.2 0.8 %collective-permute-done.9.odd3 = bf16[128,1024]{1,0:T(8,128)(2,1)S(1)} collective-permute-done((bf16[128,1024]{1,0:T(8,128)(2,1)S(1)}, bf16[128,1024]{1,0:T(8,128)(2,1)S(1)}, u32[]{:S(2)}, u32[]{:S(2)}) %collective-permute-start.9) | collective-permute-done | bytes 262176 | tf_op jit(solution)/shard_map/ppermute | solution.py:363
  30.0 1.4 %final.1 = bf16[128,1024]{1,0:T(8,128)(2,1)} custom-call(f32[4,128,128]{2,1,0:T(8,128)S(1)} %get-tuple-element.34.gate_ref, bf16[128,1024]{1,0:T(8,128)(2,1)S(1)} %get-tuple-element.35.t2_ref, f32[128,1024]{1,0:T(8,128)S(1)} %get-tuple-element.47.acc_ref, f32[128,1024]{1,0:T(8,128)S(1)} %get-tuple-element.48.top_ref, ...), custom_call_target="tpu_custom_call" | custom-call | tf_op jit(solution)/shard_map/final/pallas_call | solution.py:262
Async XLA Ops:
  0.0 7.7 %copy-start = (bf16[128,1024]{1,0:T(8,128)(2,1)S(1)}, bf16[128,1024]{1,0:T(8,128)(2,1)}, u32[]{:S(2)}) copy-start(bf16[128,1024]{1,0:T(8,128)(2,1)} %v_ref.1) | copy-start | bytes 786436
  0.0 10.6 %copy-start.1 = (s32[8192]{0:T(1024)S(1)}, s32[8192]{0:T(1024)}, u32[]{:S(2)}) copy-start(s32[8192]{0:T(1024)} %param.12) | copy-start | bytes 98308
  3.9 6.6 %collective-permute-start = (bf16[128,1024]{1,0:T(8,128)(2,1)S(1)}, bf16[128,1024]{1,0:T(8,128)(2,1)S(1)}, u32[]{:S(2)}, u32[]{:S(2)}) collective-permute-start(bf16[128,1024]{1,0:T(8,128)(2,1)S(1)} %get-tuple-element.33.d_ref), channel_id=1, source_target_pairs={{0,4},{4,0},{8,12},{12,8},{16,20},{20,16},{24,28},{28,24},{32,36},... | collective-permute-start | bytes 786440 | tf_op jit(solution)/shard_map/ppermute | solution.py:307
  4.7 11.0 %collective-permute-start.2 = (bf16[128,1024]{1,0:T(8,128)(2,1)S(1)}, bf16[128,1024]{1,0:T(8,128)(2,1)S(1)}, u32[]{:S(2)}, u32[]{:S(2)}) collective-permute-start(bf16[128,1024]{1,0:T(8,128)(2,1)S(1)} %get-tuple-element.36.c_ref), channel_id=1, source_target_pairs={{0,4},{4,8},{8,12},{12,16},{16,20},{20,24},{24,28},{28,32},{32,36}... | collective-permute-start | bytes 786440 | tf_op jit(solution)/shard_map/ppermute | solution.py:306
  7.7 9.9 %collective-permute-start.4 = (bf16[128,1024]{1,0:T(8,128)(2,1)S(1)}, bf16[128,1024]{1,0:T(8,128)(2,1)S(1)}, u32[]{:S(2)}, u32[]{:S(2)}) collective-permute-start(bf16[128,1024]{1,0:T(8,128)(2,1)S(1)} %copy-done), channel_id=1, source_target_pairs={{0,8},{4,12},{8,16},{12,20},{16,24},{20,28},{24,32},{28,36},{32,40... | collective-permute-start | bytes 786440 | tf_op jit(solution)/shard_map/ppermute | solution.py:309
  11.6 8.0 %collective-permute-start.3 = (bf16[128,1024]{1,0:T(8,128)(2,1)S(1)}, bf16[128,1024]{1,0:T(8,128)(2,1)S(1)}, u32[]{:S(2)}, u32[]{:S(2)}) collective-permute-start(bf16[128,1024]{1,0:T(8,128)(2,1)S(1)} %copy-done), channel_id=1, source_target_pairs={{4,16},{12,24},{20,32},{28,40},{36,48},{44,56},{52,64},{60,72},{68... | collective-permute-start | bytes 786440 | tf_op jit(solution)/shard_map/ppermute | solution.py:326
  15.0 6.2 %collective-permute-start.1 = (bf16[128,1024]{1,0:T(8,128)(2,1)S(1)}, bf16[128,1024]{1,0:T(8,128)(2,1)S(1)}, u32[]{:S(2)}, u32[]{:S(2)}) collective-permute-start(bf16[128,1024]{1,0:T(8,128)(2,1)S(1)} %get-tuple-element.38), channel_id=1, source_target_pairs={{0,8},{8,16},{16,24},{24,32},{32,40},{40,48},{48,56},{56,64},{64,7... | collective-permute-start | bytes 786440 | tf_op jit(solution)/shard_map/ppermute | solution.py:337
  15.9 13.2 %collective-permute-start.8 = (bf16[128,1024]{1,0:T(8,128)(2,1)S(1)}, bf16[128,1024]{1,0:T(8,128)(2,1)S(1)}, u32[]{:S(2)}, u32[]{:S(2)}) collective-permute-start(bf16[128,1024]{1,0:T(8,128)(2,1)S(1)} %third.1._), channel_id=1, source_target_pairs={{0,8},{8,16},{16,24},{24,32},{32,40},{40,48},{48,56},{56,64},{64,7... | collective-permute-start | bytes 786440 | tf_op jit(solution)/shard_map/ppermute | solution.py:345
  17.7 4.9 %collective-permute-start.5 = (bf16[128,1024]{1,0:T(8,128)(2,1)S(1)}, bf16[128,1024]{1,0:T(8,128)(2,1)S(1)}, u32[]{:S(2)}, u32[]{:S(2)}) collective-permute-start(bf16[128,1024]{1,0:T(8,128)(2,1)S(1)} %collective-permute-done.4.early_ref), channel_id=1, source_target_pairs={{0,4},{4,0},{8,12},{12,8},{16,20},{20,16},{24,28},{28,24},{32,36},... | collective-permute-start | bytes 786440 | tf_op jit(solution)/shard_map/ppermute | solution.py:360
  19.5 3.0 %collective-permute-start.6 = (bf16[128,1024]{1,0:T(8,128)(2,1)S(1)}, bf16[128,1024]{1,0:T(8,128)(2,1)S(1)}, u32[]{:S(2)}, u32[]{:S(2)}) collective-permute-start(bf16[128,1024]{1,0:T(8,128)(2,1)S(1)} %copy-done), channel_id=1, source_target_pairs={{0,4},{4,0},{8,12},{12,8},{16,20},{20,16},{24,28},{28,24},{32,36},... | collective-permute-start | bytes 786440 | tf_op jit(solution)/shard_map/ppermute | solution.py:361
  19.6 8.7 %collective-permute-start.7 = (bf16[128,1024]{1,0:T(8,128)(2,1)S(1)}, bf16[128,1024]{1,0:T(8,128)(2,1)S(1)}, u32[]{:S(2)}, u32[]{:S(2)}) collective-permute-start(bf16[128,1024]{1,0:T(8,128)(2,1)S(1)} %collective-permute-done.2.near_ref), channel_id=1, source_target_pairs={{0,4},{8,12},{16,20},{24,28},{32,36},{40,44},{48,52},{56,60},{64,6... | collective-permute-start | bytes 786440 | tf_op jit(solution)/shard_map/ppermute | solution.py:359
  21.3 8.7 %collective-permute-start.9 = (bf16[128,1024]{1,0:T(8,128)(2,1)S(1)}, bf16[128,1024]{1,0:T(8,128)(2,1)S(1)}, u32[]{:S(2)}, u32[]{:S(2)}) collective-permute-start(bf16[128,1024]{1,0:T(8,128)(2,1)S(1)} %collective-permute-done.1.even2), channel_id=1, source_target_pairs={{0,4},{8,12},{16,20},{24,28},{32,36},{40,44},{48,52},{56,60},{64,6... | collective-permute-start | bytes 786440 | tf_op jit(solution)/shard_map/ppermute | solution.py:363

commit v4 on v3

--- a/solution.py
+++ b/solution.py
@@ -11,6 +11,7 @@
 BACK = 3
 EPSILON = 1e-06
 GROUP = 4
+LAST_GROUP = 4
 F32 = jnp.float32
 BF16 = jnp.bfloat16
 SCALE = HEAD_DIM**-0.5 * math.log2(math.e)
@@ -189,7 +190,7 @@
         gate_ref[back] = jnp.where(allowed, 0.0, -1e30)
 
 
-def near_kernel(gate_ref, t_ref, own_ref, near_ref, _, __, score_ref):
+def near_kernel(gate_ref, t_ref, own_ref, near_ref, _, score_ref):
     for h in range(t_ref.shape[1] // HEAD_DIM):
         c = columns(h)
         score_ref[0, :, c] = own_ref[:, c] + gate_ref[0]
@@ -233,12 +234,12 @@
     heads = t2_ref.shape[1] // HEAD_DIM
 
     def copy(group):
-        part = slice(group * HEAD_DIM, (group + GROUP) * HEAD_DIM)
+        part = slice(group * HEAD_DIM, (group + LAST_GROUP) * HEAD_DIM)
         return pltpu.make_async_copy(out_ref.at[:, part], out_hbm.at[:, part], sems.at[group])
 
     def run(far, v3):
-        for group in range(0, heads, GROUP):
-            cs = [columns(h) for h in range(group, group + GROUP)]
+        for group in range(0, heads, LAST_GROUP):
+            cs = [columns(h) for h in range(group, group + LAST_GROUP)]
             score = [dot_nt(t2_ref[:, c], far[:, c]) + gate_ref[3] for c in cs]
             top = [
                 jnp.maximum(jnp.max(x, axis=-1, keepdims=True), top_ref[:, c])
@@ -253,7 +254,7 @@
             copy(group).start()
 
     by_parity(lambda: run(even3, direct), lambda: run(odd3, swapped))
-    for group in range(0, heads, GROUP):
+    for group in range(0, heads, LAST_GROUP):
         copy(group).wait()
 
 
@@ -351,13 +352,13 @@
         own,
         near_k,
         third,
-        direct,
-        specs=[vmem] * 4 + [anywhere] * 2,
+        specs=[vmem] * 4 + [anywhere],
         name="near",
     )
     near_k_, early_, values_, _ = lax.optimization_barrier((near_k, early, values, third))
     odd2 = lax.ppermute(near_k_, "seq", to_odd)
     swapped = lax.ppermute(early_, "seq", swap)
+    values_, direct, scores = lax.optimization_barrier((values_, direct, scores))
     pair_v = lax.ppermute(values_, "seq", swap)
     even2_, scores = lax.optimization_barrier((even2, scores))
     odd3 = lax.ppermute(even2_, "seq", to_odd)

time: 31.6 us -> 31.1 us (0.984)
  the two profiles are of different devices: /device:TPU:139 before, /device:TPU:136 now
where the time goes in v4:
time: 31.1 us; the launch traced here: 30.7 us
  starting transfers between devices  17.5 us (56%)
  Pallas kernels  8.16 us (26%)
  waiting for transfers between devices  4.91 us (16%)
    pallas_call x7, Pallas kernels, call(): pl.pallas_call(body, out_shape=outs, in_specs=specs or [kept] * len(args)...  8.16 us
    ppermute x1, starting transfers between devices, shards(): even2 = lax.ppermute(second, 'seq', next_even)  3.4 us
    ppermute x1, starting transfers between devices, shards(): early = lax.ppermute(later, 'seq', next_two)  3.39 us
    ppermute x1, starting transfers between devices, shards(): even3 = lax.ppermute(third, 'seq', next_even)  3.11 us
    ppermute x1, waiting for transfers between devices, shards(): early = lax.ppermute(later, 'seq', next_two)  2.61 us
    ppermute x1, starting transfers between devices, shards(): near_k = lax.ppermute(carried, 'seq', next_one)  2.39 us
    ppermute x1, starting transfers between devices, shards(): odd2 = lax.ppermute(near_k_, 'seq', to_odd)  2.36 us
    ppermute x1, waiting for transfers between devices, shards(): even2 = lax.ppermute(second, 'seq', next_even)  1.71 us
  transfers between devices with their start and end apart: 10, of which 3 were waited for; matrix products, arithmetic and copies ran while one was open for 0% of the time, Pallas kernels for 9%

profile of v4, /device:TPU:136, one launch (start us, length us, event | category | flops | bytes accessed | tf_op | source)
XLA Modules:
  0.0 30.7 jit_solution(9742184102868059803)
XLA Ops:
  0.0 0.0 copy-start
  0.0 0.0 copy-start.1
  0.0 3.9 %prep.1 = (bf16[128,1024]{1,0:T(8,128)(2,1)S(1)}, bf16[128,1024]{1,0:T(8,128)(2,1)S(1)}, bf16[128,1024]{1,0:T(8,128)(2,1)S(1)}, bf16[128,1024]{1,0:T(8,128)(2,1)...) custom-call(bf16[128,1024]{1,0:T(8,128)(2,1)} %k_hbm.1, ...), custom_call_target="tpu_custom_call" | custom-call | tf_op jit(solution)/shard_map/prep/pallas_call | solution.py:263
  3.9 0.1 collective-permute-start
  4.0 2.4 %collective-permute-start.2 = (bf16[128,1024]{1,0:T(8,128)(2,1)S(1)}, bf16[128,1024]{1,0:T(8,128)(2,1)S(1)}, u32[]{:S(2)}, u32[]{:S(2)}) collective-permute-start(bf16[128,1024]{1,0:T(8,128)(2,1)S(1)} %get-tuple-element.39.c_ref), channel_id=1, source_target_pairs={{0,4},{4,8},{8,12},{12,16},{16,20},{20,24},{24,28},{28,32},{32,36}... | collective-permute-start | bytes 786440 | tf_op jit(solution)/shard_map/ppermute | solution.py:307
  6.5 0.0 copy-done
  6.5 3.4 %collective-permute-start.3 = (bf16[128,1024]{1,0:T(8,128)(2,1)S(1)}, bf16[128,1024]{1,0:T(8,128)(2,1)S(1)}, u32[]{:S(2)}, u32[]{:S(2)}) collective-permute-start(bf16[128,1024]{1,0:T(8,128)(2,1)S(1)} %copy-done), channel_id=1, source_target_pairs={{0,8},{4,12},{8,16},{12,20},{16,24},{20,28},{24,32},{28,36},{32,40... | collective-permute-start | bytes 786440 | tf_op jit(solution)/shard_map/ppermute | solution.py:310
  9.9 0.0 collective-permute-done.other_ref
  9.9 0.0 copy-done.1
  9.9 1.0 %query.1 = (bf16[128,1024]{1,0:T(8,128)(2,1)S(1)}, bf16[128,1024]{1,0:T(8,128)(2,1)S(1)}, f32[128,1024]{1,0:T(8,128)S(1)}, f32[4,128,128]{2,1,0:T(8,128)S(1)}) custom-call(s32[1,3]{1,0:T(1,128)} %visits_hbm.1, s32[64,128]{1,0:T(8,128)S(1)} %bitcast.2, bf16[128,1024]{1,0:T(8,128)(2,1)S(1)} %get-tuple-element.31.q_ref, ...), custom_call_target="tpu_custom_call" | custom-call | tf_op jit(solution)/shard_map/query/pallas_call | solution.py:263
  10.9 1.3 %collective-permute-start.4 = (bf16[128,1024]{1,0:T(8,128)(2,1)S(1)}, bf16[128,1024]{1,0:T(8,128)(2,1)S(1)}, u32[]{:S(2)}, u32[]{:S(2)}) collective-permute-start(bf16[128,1024]{1,0:T(8,128)(2,1)S(1)} %copy-done), channel_id=1, source_target_pairs={{4,16},{12,24},{20,32},{28,40},{36,48},{44,56},{52,64},{60,72},{68... | collective-permute-start | bytes 786440 | tf_op jit(solution)/shard_map/ppermute | solution.py:327
  12.2 0.3 pair.1
  12.5 3.4 %collective-permute-start.1 = (bf16[128,1024]{1,0:T(8,128)(2,1)S(1)}, bf16[128,1024]{1,0:T(8,128)(2,1)S(1)}, u32[]{:S(2)}, u32[]{:S(2)}) collective-permute-start(bf16[128,1024]{1,0:T(8,128)(2,1)S(1)} %get-tuple-element.41), channel_id=1, source_target_pairs={{0,8},{8,16},{16,24},{24,32},{32,40},{40,48},{48,56},{56,64},{64,7... | collective-permute-start | bytes 786440 | tf_op jit(solution)/shard_map/ppermute | solution.py:338
  15.9 0.0 collective-permute-done.2.near_ref
  15.9 0.2 third.1._
  16.2 3.1 %collective-permute-start.8 = (bf16[128,1024]{1,0:T(8,128)(2,1)S(1)}, bf16[128,1024]{1,0:T(8,128)(2,1)S(1)}, u32[]{:S(2)}, u32[]{:S(2)}) collective-permute-start(bf16[128,1024]{1,0:T(8,128)(2,1)S(1)} %third.1._), channel_id=1, source_target_pairs={{0,8},{8,16},{16,24},{24,32},{32,40},{40,48},{48,56},{56,64},{64,7... | collective-permute-start | bytes 786440 | tf_op jit(solution)/shard_map/ppermute | solution.py:346
  19.3 2.6 %collective-permute-done.3.early_ref = bf16[128,1024]{1,0:T(8,128)(2,1)S(1)} collective-permute-done((bf16[128,1024]{1,0:T(8,128)(2,1)S(1)}, bf16[128,1024]{1,0:T(8,128)(2,1)S(1)}, u32[]{:S(2)}, u32[]{:S(2)}) %collective-permute-start.3) | collective-permute-done | bytes 262176 | tf_op jit(solution)/shard_map/ppermute | solution.py:310
  21.9 0.1 collective-permute-start.5
  22.0 2.4 %collective-permute-start.7 = (bf16[128,1024]{1,0:T(8,128)(2,1)S(1)}, bf16[128,1024]{1,0:T(8,128)(2,1)S(1)}, u32[]{:S(2)}, u32[]{:S(2)}) collective-permute-start(bf16[128,1024]{1,0:T(8,128)(2,1)S(1)} %collective-permute-done.2.near_ref), channel_id=1, source_target_pairs={{0,4},{8,12},{16,20},{24,28},{32,36},{40,44},{48,52},{56,60},{64,6... | collective-permute-start | bytes 786440 | tf_op jit(solution)/shard_map/ppermute | solution.py:359
  24.3 0.3 %near.1.score_ref = f32[2,128,1024]{2,1,0:T(8,128)S(1)} custom-call(f32[4,128,128]{2,1,0:T(8,128)S(1)} %get-tuple-element.37.gate_ref, bf16[128,1024]{1,0:T(8,128)(2,1)S(1)} %get-tuple-element.40._.t_ref, f32[128,1024]{1,0:T(8,128)S(1)} %get-tuple-element.46.own_ref, bf16[128,1024]{1,0:T(8,128)(2,1)S(1)} %collective-permute-done.2.near_ref, ...), custom_call_target="tpu_custom_call" | custom-call | tf_op jit(solution)/shard_map/near/pallas_call | solution.py:263
  24.6 0.0 collective-permute-done.4.direct
  24.7 0.1 collective-permute-start.6
  24.8 1.7 %collective-permute-done.1.even2 = bf16[128,1024]{1,0:T(8,128)(2,1)S(1)} collective-permute-done((bf16[128,1024]{1,0:T(8,128)(2,1)S(1)}, bf16[128,1024]{1,0:T(8,128)(2,1)S(1)}, u32[]{:S(2)}, u32[]{:S(2)}) %collective-permute-start.1) | collective-permute-done | bytes 262176 | tf_op jit(solution)/shard_map/ppermute | solution.py:338
  26.5 1.3 %collective-permute-start.9 = (bf16[128,1024]{1,0:T(8,128)(2,1)S(1)}, bf16[128,1024]{1,0:T(8,128)(2,1)S(1)}, u32[]{:S(2)}, u32[]{:S(2)}) collective-permute-start(bf16[128,1024]{1,0:T(8,128)(2,1)S(1)} %collective-permute-done.1.even2), channel_id=1, source_target_pairs={{0,4},{8,12},{16,20},{24,28},{32,36},{40,44},{48,52},{56,60},{64,6... | collective-permute-start | bytes 786440 | tf_op jit(solution)/shard_map/ppermute | solution.py:364
  27.8 0.0 collective-permute-done.5.swapped_ref.swapped
  27.8 0.0 collective-permute-done.7.odd2
  27.8 0.0 collective-permute-done.6.pair_v_ref
  27.8 0.9 %mid.1 = (f32[128,1024]{1,0:T(8,128)S(1)}, f32[128,1024]{1,0:T(8,128)S(1)}, f32[128,1024]{1,0:T(8,128)S(1)}) custom-call(f32[4,128,128]{2,1,0:T(8,128)S(1)} %get-tuple-element.37.gate_ref, bf16[128,1024]{1,0:T(8,128)(2,1)S(1)} %get-tuple-element.38.t2_ref, f32[2,128,1024]{2,1,0:T(8,128)S(1)} %near.1.score_ref, bf16[128,1024]{1,0:T(8,128)(2,1)S(1)} %copy-done, ...), custom_call_target="tpu_custom_call" | custom-call | tf_op jit(solution)/shard_map/mid/pallas_call | solution.py:263
  28.7 0.6 %collective-permute-done.8.even3 = bf16[128,1024]{1,0:T(8,128)(2,1)S(1)} collective-permute-done((bf16[128,1024]{1,0:T(8,128)(2,1)S(1)}, bf16[128,1024]{1,0:T(8,128)(2,1)S(1)}, u32[]{:S(2)}, u32[]{:S(2)}) %collective-permute-start.8) | collective-permute-done | bytes 262176 | tf_op jit(solution)/shard_map/ppermute | solution.py:346
  29.3 0.0 collective-permute-done.9.odd3
  29.3 1.4 %final.1 = bf16[128,1024]{1,0:T(8,128)(2,1)} custom-call(f32[4,128,128]{2,1,0:T(8,128)S(1)} %get-tuple-element.37.gate_ref, bf16[128,1024]{1,0:T(8,128)(2,1)S(1)} %get-tuple-element.38.t2_ref, f32[128,1024]{1,0:T(8,128)S(1)} %get-tuple-element.52.acc_ref, f32[128,1024]{1,0:T(8,128)S(1)} %get-tuple-element.53.top_ref, ...), custom_call_target="tpu_custom_call" | custom-call | tf_op jit(solution)/shard_map/final/pallas_call | solution.py:263
Async XLA Ops:
  0.0 6.5 %copy-start = (bf16[128,1024]{1,0:T(8,128)(2,1)S(1)}, bf16[128,1024]{1,0:T(8,128)(2,1)}, u32[]{:S(2)}) copy-start(bf16[128,1024]{1,0:T(8,128)(2,1)} %v_ref.1) | copy-start | bytes 786436
  0.0 9.9 %copy-start.1 = (s32[8192]{0:T(1024)S(1)}, s32[8192]{0:T(1024)}, u32[]{:S(2)}) copy-start(s32[8192]{0:T(1024)} %param.12) | copy-start | bytes 98308
  3.9 5.9 %collective-permute-start = (bf16[128,1024]{1,0:T(8,128)(2,1)S(1)}, bf16[128,1024]{1,0:T(8,128)(2,1)S(1)}, u32[]{:S(2)}, u32[]{:S(2)}) collective-permute-start(bf16[128,1024]{1,0:T(8,128)(2,1)S(1)} %get-tuple-element.36.d_ref), channel_id=1, source_target_pairs={{0,4},{4,0},{8,12},{12,8},{16,20},{20,16},{24,28},{28,24},{32,36},... | collective-permute-start | bytes 786440 | tf_op jit(solution)/shard_map/ppermute | solution.py:308
  4.0 11.9 %collective-permute-start.2 = (bf16[128,1024]{1,0:T(8,128)(2,1)S(1)}, bf16[128,1024]{1,0:T(8,128)(2,1)S(1)}, u32[]{:S(2)}, u32[]{:S(2)}) collective-permute-start(bf16[128,1024]{1,0:T(8,128)(2,1)S(1)} %get-tuple-element.39.c_ref), channel_id=1, source_target_pairs={{0,4},{4,8},{8,12},{12,16},{16,20},{20,24},{24,28},{28,32},{32,36}... | collective-permute-start | bytes 786440 | tf_op jit(solution)/shard_map/ppermute | solution.py:307
  6.5 15.4 %collective-permute-start.3 = (bf16[128,1024]{1,0:T(8,128)(2,1)S(1)}, bf16[128,1024]{1,0:T(8,128)(2,1)S(1)}, u32[]{:S(2)}, u32[]{:S(2)}) collective-permute-start(bf16[128,1024]{1,0:T(8,128)(2,1)S(1)} %copy-done), channel_id=1, source_target_pairs={{0,8},{4,12},{8,16},{12,20},{16,24},{20,28},{24,32},{28,36},{32,40... | collective-permute-start | bytes 786440 | tf_op jit(solution)/shard_map/ppermute | solution.py:310
  10.9 13.7 %collective-permute-start.4 = (bf16[128,1024]{1,0:T(8,128)(2,1)S(1)}, bf16[128,1024]{1,0:T(8,128)(2,1)S(1)}, u32[]{:S(2)}, u32[]{:S(2)}) collective-permute-start(bf16[128,1024]{1,0:T(8,128)(2,1)S(1)} %copy-done), channel_id=1, source_target_pairs={{4,16},{12,24},{20,32},{28,40},{36,48},{44,56},{52,64},{60,72},{68... | collective-permute-start | bytes 786440 | tf_op jit(solution)/shard_map/ppermute | solution.py:327
  12.5 14.0 %collective-permute-start.1 = (bf16[128,1024]{1,0:T(8,128)(2,1)S(1)}, bf16[128,1024]{1,0:T(8,128)(2,1)S(1)}, u32[]{:S(2)}, u32[]{:S(2)}) collective-permute-start(bf16[128,1024]{1,0:T(8,128)(2,1)S(1)} %get-tuple-element.41), channel_id=1, source_target_pairs={{0,8},{8,16},{16,24},{24,32},{32,40},{40,48},{48,56},{56,64},{64,7... | collective-permute-start | bytes 786440 | tf_op jit(solution)/shard_map/ppermute | solution.py:338
  16.2 13.1 %collective-permute-start.8 = (bf16[128,1024]{1,0:T(8,128)(2,1)S(1)}, bf16[128,1024]{1,0:T(8,128)(2,1)S(1)}, u32[]{:S(2)}, u32[]{:S(2)}) collective-permute-start(bf16[128,1024]{1,0:T(8,128)(2,1)S(1)} %third.1._), channel_id=1, source_target_pairs={{0,8},{8,16},{16,24},{24,32},{32,40},{40,48},{48,56},{56,64},{64,7... | collective-permute-start | bytes 786440 | tf_op jit(solution)/shard_map/ppermute | solution.py:346
  21.9 5.9 %collective-permute-start.5 = (bf16[128,1024]{1,0:T(8,128)(2,1)S(1)}, bf16[128,1024]{1,0:T(8,128)(2,1)S(1)}, u32[]{:S(2)}, u32[]{:S(2)}) collective-permute-start(bf16[128,1024]{1,0:T(8,128)(2,1)S(1)} %collective-permute-done.3.early_ref), channel_id=1, source_target_pairs={{0,4},{4,0},{8,12},{12,8},{16,20},{20,16},{24,28},{28,24},{32,36},... | collective-permute-start | bytes 786440 | tf_op jit(solution)/shard_map/ppermute | solution.py:360
  22.0 5.8 %collective-permute-start.7 = (bf16[128,1024]{1,0:T(8,128)(2,1)S(1)}, bf16[128,1024]{1,0:T(8,128)(2,1)S(1)}, u32[]{:S(2)}, u32[]{:S(2)}) collective-permute-start(bf16[128,1024]{1,0:T(8,128)(2,1)S(1)} %collective-permute-done.2.near_ref), channel_id=1, source_target_pairs={{0,4},{8,12},{16,20},{24,28},{32,36},{40,44},{48,52},{56,60},{64,6... | collective-permute-start | bytes 786440 | tf_op jit(solution)/shard_map/ppermute | solution.py:359
  24.7 3.1 %collective-permute-start.6 = (bf16[128,1024]{1,0:T(8,128)(2,1)S(1)}, bf16[128,1024]{1,0:T(8,128)(2,1)S(1)}, u32[]{:S(2)}, u32[]{:S(2)}) collective-permute-start(bf16[128,1024]{1,0:T(8,128)(2,1)S(1)} %copy-done), channel_id=1, source_target_pairs={{0,4},{4,0},{8,12},{12,8},{16,20},{20,16},{24,28},{28,24},{32,36},... | collective-permute-start | bytes 786440 | tf_op jit(solution)/shard_map/ppermute | solution.py:362
  26.5 2.8 %collective-permute-start.9 = (bf16[128,1024]{1,0:T(8,128)(2,1)S(1)}, bf16[128,1024]{1,0:T(8,128)(2,1)S(1)}, u32[]{:S(2)}, u32[]{:S(2)}) collective-permute-start(bf16[128,1024]{1,0:T(8,128)(2,1)S(1)} %collective-permute-done.1.even2), channel_id=1, source_target_pairs={{0,4},{8,12},{16,20},{24,28},{32,36},{40,44},{48,52},{56,60},{64,6... | collective-permute-start | bytes 786440 | tf_op jit(solution)/shard_map/ppermute | solution.py:364
